TPU v7x, 32 devices: a whole 2x2x4 slice. The times are simulated.
32 devices in a mesh: seq: 8 (over z, x), tier: 4 (over y, core).
Axes of the slice: x: 2, y: 2, z: 4, core: 2. Of those that a mesh axis runs over, the one named last changes fastest.
Arguments:
- layer_input: bfloat16 [8, 512, 1024], P('seq', 'tier'), may hold values from -6 to 6
- memory: bfloat16 [8, 512, 1024], P('seq', 'tier'), may hold values from -6 to 6
- compressed: bfloat16 [8, 512, 1024], P('seq', 'tier'), may hold values from -6 to 6
- seg_len: int32 [8], P('seq'), may hold values from 1 to 512, as said below
- hist_len: int32 [8], P('seq'), may hold values from 0 to 1024, as said below
- query_weight: bfloat16 [1024, 1024], replicated, may hold values from -0.1875 to 0.1875
- key_weight: bfloat16 [1024, 1024], replicated, may hold values from -0.1875 to 0.1875
- value_weight: bfloat16 [1024, 1024], replicated, may hold values from -0.1875 to 0.1875
- attn_out_weight: bfloat16 [1024, 1024], replicated, may hold values from -1 to 1
- ffn_in_weight: bfloat16 [1024, 4096], replicated, may hold values from -0.1875 to 0.1875
- ffn_out_weight: bfloat16 [4096, 1024], replicated, may hold values from -0.09375 to 0.09375
- norm_gain: float32 [1024], replicated, may hold values from 0.1 to 1.9
- head_slope: float32 [8], replicated, may hold values from 0.0005 to 0.05
- comp_weight: bfloat16 [3072, 1024], replicated, may hold values from -0.109375 to 0.109375
- cotangent: bfloat16 [8, 512, 1024], P('seq', 'tier'), may hold values from -6 to 6
Outputs:
- output: bfloat16 [8, 512, 1024], P('seq', 'tier')
- grad_input: float32 [8, 512, 1024], P('seq', 'tier')
- new_memory: bfloat16 [8, 512, 1024], P('seq', 'tier')
- new_compressed: bfloat16 [8, 512, 1024], P('seq', 'tier')
- grad_query_weight: float32 [1024, 1024], P('seq', 'tier')
- grad_key_weight: float32 [1024, 1024], P('seq', 'tier')
- grad_value_weight: float32 [1024, 1024], P('seq', 'tier')
- grad_attn_out_weight: float32 [1024, 1024], P('seq', 'tier')
- grad_ffn_in_weight: float32 [1024, 4096], P('seq', 'tier')
- grad_ffn_out_weight: float32 [4096, 1024], P('seq', 'tier')
- grad_comp_weight: float32 [3072, 1024], P('seq', 'tier')
- grad_norm_gain: float32 [1024], replicated
- grad_head_slope: float32 [8], replicated
Inputs may be any that keep to these rules, and one draw needn't show every extreme that they name: `seg_len`: the first sequence's segment is full; others may end early, as the last segment of a book does. `hist_len`: the first sequence has a full history; a book's early segments have a short one.
All inputs are finite; a program needn't handle non-finite values.
Results may differ from a plain program's by a relative error of at most 0.014.
Values may be sent and summed in bfloat16 or wider, within the bound.
A program may use at most 256 MiB of HBM per device.

v0:
```python
import functools
import math

import jax
import jax.numpy as jnp
from jax import lax
from jax.experimental import pallas as pl
from jax.experimental.pallas import tpu as pltpu
from jax.sharding import PartitionSpec as P

norm_eps = 1e-05
neg_large = -1e30
f32 = jnp.float32
bf16 = jnp.bfloat16


def gelu_tanh(values_in):
    return jax.nn.gelu(values_in, approximate=True)


def layer_norm(residual, norm_gain):
    centre = jnp.mean(residual, axis=-1, keepdims=True)
    deviation = residual - centre
    variance = jnp.mean(deviation * deviation, axis=-1, keepdims=True)
    return deviation * lax.rsqrt(variance + norm_eps) * norm_gain


def softmax_grad(weights, grad_weights):
    inner_sum = jnp.sum(weights * grad_weights, axis=-1, keepdims=True)
    return (weights * (grad_weights - inner_sum)).astype(bf16)


def mm(left, right):
    return jnp.dot(left, right, preferred_element_type=f32)


def mm_tn(left, right):
    return lax.dot_general(left, right, (((0,), (0,)), ((), ())), preferred_element_type=f32)


def mm_nt(left, right):
    return lax.dot_general(left, right, (((1,), (1,)), ((), ())), preferred_element_type=f32)


MESH = pl.DeviceIdType.MESH


def ring_seq(pos, seqs):
    half = seqs // 2
    col = pos // half
    row = pos - col * (2 * pos - 2 * half + 1)
    return 2 * row + col


def ring_pos(idx, seqs):
    half = seqs // 2
    row = idx // 2
    col = idx - 2 * row
    return row + col * (2 * half - 1 - 2 * row)


def ring_rs_kernel(seqs, tiers, nparts, *refs):
    x_refs = refs[:nparts]
    g_ref = refs[nparts]
    out_refs = refs[nparts + 1 : 2 * nparts + 1]
    gout_ref = refs[2 * nparts + 1]
    scratch = refs[2 * nparts + 2 :]
    recvs = scratch[:nparts]
    sbufs = scratch[nparts : 2 * nparts]
    (send_sem, recv_sem, free_sem, grecv, gsbuf, gsend_sem, grecv_sem, gfree_sem,
     tsrc, trecv, tsend_sem, trecv_sem) = scratch[2 * nparts :]

    me = lax.axis_index("seq")
    tier = lax.axis_index("tier")
    pos = ring_pos(me, seqs)
    nbr = (ring_seq(lax.rem(pos + 1, seqs), seqs), ring_seq(lax.rem(pos + seqs - 1, seqs), seqs))

    barrier = pltpu.get_barrier_semaphore()
    for d in range(2):
        pl.semaphore_signal(barrier, inc=1, device_id=(nbr[d], tier), device_id_type=MESH)
    for j in range(1, tiers):
        peer = lax.rem(tier + j, tiers)
        pl.semaphore_signal(barrier, inc=1, device_id=(me, peer), device_id_type=MESH)
    pl.semaphore_wait(barrier, 2 + tiers - 1)

    tcopies = []
    for j in range(1, tiers):
        peer = lax.rem(tier + j, tiers)
        cp = pltpu.make_async_remote_copy(
            src_ref=g_ref,
            dst_ref=trecv.at[j - 1],
            send_sem=tsend_sem.at[j - 1],
            recv_sem=trecv_sem.at[j - 1],
            device_id=(me, peer),
            device_id_type=MESH,
        )
        cp.start()
        tcopies.append(cp)
    tier_sum = g_ref[...]
    for j, cp in enumerate(tcopies):
        cp.wait()
        tier_sum = tier_sum + trecv[j]
    tsrc[...] = tier_sum

    def block_of(d, k):
        if d == 0:
            return ring_seq(lax.rem(pos - k - 1 + 2 * seqs, seqs), seqs)
        return ring_seq(lax.rem(pos + k + 1, seqs), seqs)

    def window(i, d, blk):
        rows, cols = out_refs[i].shape
        half = cols // 2
        return x_refs[i].at[pl.ds(pl.multiple_of(blk * rows, rows), rows), pl.ds(d * half, half)]

    copies = {}
    for k in range(seqs - 1):
        slot = k % 2
        for d in range(2):
            blk = block_of(d, k)
            if k > 0:
                for i in range(nparts):
                    copies[i, d].wait_recv()
                    sbufs[i][d, slot] = (
                        recvs[i][d, 1 - slot].astype(f32) + window(i, d, blk)[...].astype(f32)
                    ).astype(bf16)
                if k <= seqs - 3:
                    pl.semaphore_signal(free_sem.at[d], inc=1, device_id=(nbr[1 - d], tier), device_id_type=MESH)
            if k >= 2:
                pl.semaphore_wait(free_sem.at[d], 1)
            for i in range(nparts):
                copies[i, d] = pltpu.make_async_remote_copy(
                    src_ref=window(i, d, blk) if k == 0 else sbufs[i].at[d, slot],
                    dst_ref=recvs[i].at[d, slot],
                    send_sem=send_sem.at[i, d, slot],
                    recv_sem=recv_sem.at[i, d, slot],
                    device_id=(nbr[d], tier),
                    device_id_type=MESH,
                )
                copies[i, d].start()
        if k > 0:
            copies["g"].wait_recv()
            gsbuf[slot] = grecv[1 - slot] + tier_sum
            if k <= seqs - 3:
                pl.semaphore_signal(gfree_sem.at[0], inc=1, device_id=(nbr[1], tier), device_id_type=MESH)
        if k >= 2:
            pl.semaphore_wait(gfree_sem.at[0], 1)
        copies["g"] = pltpu.make_async_remote_copy(
            src_ref=tsrc if k == 0 else gsbuf.at[slot],
            dst_ref=grecv.at[slot],
            send_sem=gsend_sem.at[slot],
            recv_sem=grecv_sem.at[slot],
            device_id=(nbr[0], tier),
            device_id_type=MESH,
        )
        copies["g"].start()
        for cp in copies.values():
            cp.wait_send()
    last = (seqs - 2) % 2
    for d in range(2):
        for i in range(nparts):
            copies[i, d].wait_recv()
            cols = out_refs[i].shape[1]
            half = cols // 2
            out_refs[i][:, pl.ds(d * half, half)] = (
                recvs[i][d, last].astype(f32) + window(i, d, me)[...].astype(f32)
            )
    copies["g"].wait_recv()
    gout_ref[...] = grecv[last] + tier_sum


def ring_reduce_scatter(parts, small, seqs, tiers):
    nparts = len(parts)
    shapes = [(p.shape[0] // seqs, p.shape[1]) for p in parts]
    return pl.pallas_call(
        functools.partial(ring_rs_kernel, seqs, tiers, nparts),
        out_shape=tuple(jax.ShapeDtypeStruct(sh, f32) for sh in shapes)
        + (jax.ShapeDtypeStruct(small.shape, f32),),
        in_specs=[pl.BlockSpec(memory_space=pltpu.VMEM)] * (nparts + 1),
        out_specs=(pl.BlockSpec(memory_space=pltpu.VMEM),) * (nparts + 1),
        scratch_shapes=[pltpu.VMEM((2, 2, r, c // 2), bf16) for r, c in shapes]
        + [pltpu.VMEM((2, 2, r, c // 2), bf16) for r, c in shapes]
        + [
            pltpu.SemaphoreType.DMA((nparts, 2, 2)),
            pltpu.SemaphoreType.DMA((nparts, 2, 2)),
            pltpu.SemaphoreType.REGULAR((2,)),
            pltpu.VMEM((2,) + small.shape, f32),
            pltpu.VMEM((2,) + small.shape, f32),
            pltpu.SemaphoreType.DMA((2,)),
            pltpu.SemaphoreType.DMA((2,)),
            pltpu.SemaphoreType.REGULAR((1,)),
            pltpu.VMEM(small.shape, f32),
            pltpu.VMEM((tiers - 1,) + small.shape, f32),
            pltpu.SemaphoreType.DMA((tiers - 1,)),
            pltpu.SemaphoreType.DMA((tiers - 1,)),
        ],
        compiler_params=pltpu.CompilerParams(
            collective_id=0, has_side_effects=True, vmem_limit_bytes=48 * 1024 * 1024
        ),
    )(*parts, small)


def ring_mm_kernel(seqs, tiers, plan, nfac, *refs):
    nparts = len(plan)
    facs = refs[:nfac]
    g_ref = refs[nfac]
    out_refs = refs[nfac + 1 : nfac + 1 + nparts]
    gout_ref = refs[nfac + 1 + nparts]
    scratch = refs[nfac + 2 + nparts :]
    recvs = scratch[:nparts]
    sbufs = scratch[nparts : 2 * nparts]
    owns = scratch[2 * nparts : 3 * nparts]
    (send_sem, recv_sem, free_sem, grecv, gsbuf, gsend_sem, grecv_sem, gfree_sem,
     tsrc, trecv, tsend_sem, trecv_sem) = scratch[3 * nparts :]

    me = lax.axis_index("seq")
    tier = lax.axis_index("tier")
    pos = ring_pos(me, seqs)
    nbr = (ring_seq(lax.rem(pos + 1, seqs), seqs), ring_seq(lax.rem(pos + seqs - 1, seqs), seqs))

    barrier = pltpu.get_barrier_semaphore()
    for d in range(2):
        pl.semaphore_signal(barrier, inc=1, device_id=(nbr[d], tier), device_id_type=MESH)
    for j in range(1, tiers):
        peer = lax.rem(tier + j, tiers)
        pl.semaphore_signal(barrier, inc=1, device_id=(me, peer), device_id_type=MESH)
    pl.semaphore_wait(barrier, 2 + tiers - 1)

    tcopies = []
    for j in range(1, tiers):
        peer = lax.rem(tier + j, tiers)
        cp = pltpu.make_async_remote_copy(
            src_ref=g_ref,
            dst_ref=trecv.at[j - 1],
            send_sem=tsend_sem.at[j - 1],
            recv_sem=trecv_sem.at[j - 1],
            device_id=(me, peer),
            device_id_type=MESH,
        )
        cp.start()
        tcopies.append(cp)

    def block_of(d, k):
        if k == seqs - 1:
            return me
        if d == 0:
            return ring_seq(lax.rem(pos - k - 1 + 2 * seqs, seqs), seqs)
        return ring_seq(lax.rem(pos + k + 1, seqs), seqs)

    def compute_own(k):
        for d in range(2):
            blk = block_of(d, k)
            for i, (ai, bi) in enumerate(plan):
                rows, cols = out_refs[i].shape
                half = cols // 2
                a_blk = facs[ai][:, pl.ds(pl.multiple_of(blk * rows, rows), rows)]
                b_half = facs[bi][:, pl.ds(d * half, half)]
                owns[i][d] = lax.dot_general(
                    a_blk, b_half, (((0,), (0,)), ((), ())), preferred_element_type=f32
                )

    compute_own(0)
    tier_sum = g_ref[...]
    for j, cp in enumerate(tcopies):
        cp.wait()
        tier_sum = tier_sum + trecv[j]
    tsrc[...] = tier_sum

    copies = {}
    for k in range(seqs - 1):
        slot = k % 2
        for d in range(2):
            for i in range(nparts):
                if k > 0:
                    copies[i, d].wait_recv()
                    sbufs[i][d, slot] = (recvs[i][d, 1 - slot].astype(f32) + owns[i][d]).astype(bf16)
                else:
                    sbufs[i][d, slot] = owns[i][d].astype(bf16)
            if 0 < k <= seqs - 3:
                pl.semaphore_signal(free_sem.at[d], inc=1, device_id=(nbr[1 - d], tier), device_id_type=MESH)
            if k >= 2:
                pl.semaphore_wait(free_sem.at[d], 1)
            for i in range(nparts):
                copies[i, d] = pltpu.make_async_remote_copy(
                    src_ref=sbufs[i].at[d, slot],
                    dst_ref=recvs[i].at[d, slot],
                    send_sem=send_sem.at[i, d, slot],
                    recv_sem=recv_sem.at[i, d, slot],
                    device_id=(nbr[d], tier),
                    device_id_type=MESH,
                )
                copies[i, d].start()
        if k > 0:
            copies["g"].wait_recv()
            gsbuf[slot] = grecv[1 - slot] + tier_sum
            if k <= seqs - 3:
                pl.semaphore_signal(gfree_sem.at[0], inc=1, device_id=(nbr[1], tier), device_id_type=MESH)
        if k >= 2:
            pl.semaphore_wait(gfree_sem.at[0], 1)
        copies["g"] = pltpu.make_async_remote_copy(
            src_ref=tsrc if k == 0 else gsbuf.at[slot],
            dst_ref=grecv.at[slot],
            send_sem=gsend_sem.at[slot],
            recv_sem=grecv_sem.at[slot],
            device_id=(nbr[0], tier),
            device_id_type=MESH,
        )
        copies["g"].start()
        compute_own(k + 1)
        for cp in copies.values():
            cp.wait_send()
    last = (seqs - 2) % 2
    for d in range(2):
        for i in range(nparts):
            copies[i, d].wait_recv()
            half = out_refs[i].shape[1] // 2
            out_refs[i][:, pl.ds(d * half, half)] = recvs[i][d, last].astype(f32) + owns[i][d]
    copies["g"].wait_recv()
    gout_ref[...] = grecv[last] + tier_sum


def ring_matmul_reduce(factors, plan, small, seqs, tiers):
    nfac = len(factors)
    shapes = [(factors[a].shape[1] // seqs, factors[b].shape[1]) for a, b in plan]
    nparts = len(plan)
    return pl.pallas_call(
        functools.partial(ring_mm_kernel, seqs, tiers, tuple(plan), nfac),
        out_shape=tuple(jax.ShapeDtypeStruct(sh, f32) for sh in shapes)
        + (jax.ShapeDtypeStruct(small.shape, f32),),
        in_specs=[pl.BlockSpec(memory_space=pltpu.VMEM)] * (nfac + 1),
        out_specs=(pl.BlockSpec(memory_space=pltpu.VMEM),) * (nparts + 1),
        scratch_shapes=[pltpu.VMEM((2, 2, r, c // 2), bf16) for r, c in shapes]
        + [pltpu.VMEM((2, 2, r, c // 2), bf16) for r, c in shapes]
        + [pltpu.VMEM((2, r, c // 2), f32) for r, c in shapes]
        + [
            pltpu.SemaphoreType.DMA((nparts, 2, 2)),
            pltpu.SemaphoreType.DMA((nparts, 2, 2)),
            pltpu.SemaphoreType.REGULAR((2,)),
            pltpu.VMEM((2,) + small.shape, f32),
            pltpu.VMEM((2,) + small.shape, f32),
            pltpu.SemaphoreType.DMA((2,)),
            pltpu.SemaphoreType.DMA((2,)),
            pltpu.SemaphoreType.REGULAR((1,)),
            pltpu.VMEM(small.shape, f32),
            pltpu.VMEM((tiers - 1,) + small.shape, f32),
            pltpu.SemaphoreType.DMA((tiers - 1,)),
            pltpu.SemaphoreType.DMA((tiers - 1,)),
        ],
        compiler_params=pltpu.CompilerParams(
            collective_id=1, has_side_effects=True, vmem_limit_bytes=56 * 1024 * 1024
        ),
    )(*factors, small)


def per_device(
    layer_input,
    memory,
    compressed,
    seg_len,
    hist_len,
    query_weight,
    key_weight,
    value_weight,
    attn_out_weight,
    ffn_in_weight,
    ffn_out_weight,
    norm_gain,
    head_slope,
    comp_weight,
    cotangent,
):
    _, row_count, width = layer_input.shape
    tiers = lax.axis_size("tier")
    seqs = lax.axis_size("seq")
    tier_pos = lax.axis_index("tier")
    heads = head_slope.shape[0]
    head_dim = width // heads
    hpt = heads // tiers
    cb = hpt * head_dim
    ff = ffn_in_weight.shape[1]
    ffb = ff // tiers
    seg = row_count * tiers
    keys_n = 3 * seg
    ncomp = (seg + 2) // 3
    inv_root = 1.0 / math.sqrt(head_dim)
    length = seg_len[0]
    history = hist_len[0]

    own_ids = tier_pos * row_count + jnp.arange(row_count, dtype=jnp.int32)
    mask_own = (own_ids < length).astype(f32)[:, None]
    all_ids = jnp.arange(seg, dtype=jnp.int32)
    mask_all = (all_ids < length).astype(f32)[:, None]

    hidden_own = (layer_input[0].astype(f32) * mask_own).astype(bf16)
    raw_local = jnp.stack([compressed[0], memory[0], hidden_own], axis=0)
    raw_seq = lax.all_gather(raw_local, "tier", axis=1, tiled=True)
    cot_local, raw_seq = lax.optimization_barrier((cotangent[0], raw_seq))
    cot_seq = lax.all_gather(cot_local, "tier", axis=0, tiled=True)
    context = raw_seq.reshape(keys_n, width)
    comp_rows = raw_seq[0]
    memory_rows = raw_seq[1]
    hidden_seq = raw_seq[2]

    col0 = tier_pos * cb
    wq_t = lax.dynamic_slice_in_dim(query_weight, col0, cb, axis=1)
    wk_t = lax.dynamic_slice_in_dim(key_weight, col0, cb, axis=1)
    wv_t = lax.dynamic_slice_in_dim(value_weight, col0, cb, axis=1)
    wkv_t = jnp.concatenate([wk_t, wv_t], axis=1)
    slope_t = lax.dynamic_slice_in_dim(head_slope, tier_pos * hpt, hpt)

    q_t = mm(hidden_seq, wq_t).astype(bf16)
    kv_t = mm(context, wkv_t).astype(bf16)
    q_h = q_t.reshape(seg, hpt, head_dim)
    k_h = kv_t[:, :cb].reshape(keys_n, hpt, head_dim)
    v_h = kv_t[:, cb:].reshape(keys_n, hpt, head_dim)

    key_ids = jnp.arange(keys_n, dtype=jnp.int32)
    offsets = (2 * seg + all_ids)[:, None] - key_ids[None, :]
    distance = offsets.astype(f32)
    in_history = (key_ids[None, :] < 2 * seg) & (key_ids[None, :] >= 2 * seg - history)
    in_segment = (key_ids[None, :] >= 2 * seg) & (offsets >= 0)
    key_valid = (in_history | in_segment)[None]
    scores = jnp.einsum("rhd,khd->hrk", q_h, k_h, preferred_element_type=f32) * inv_root
    scores = scores - slope_t[:, None, None] * distance[None]
    masked = jnp.where(key_valid, scores, neg_large)
    log_total = jax.nn.logsumexp(masked, axis=-1, keepdims=True)
    probs = jnp.exp(masked - log_total)
    probs_low = probs.astype(bf16)
    attended_t = jnp.einsum("hrk,khd->rhd", probs_low, v_h, preferred_element_type=f32)
    attended_t = attended_t.reshape(seg, cb).astype(bf16)
    attended = lax.all_to_all(attended_t, "tier", 0, 1, tiled=True)

    mem_k = k_h[seg : 2 * seg]
    mem_v = v_h[seg : 2 * seg]
    mem_scores = jnp.einsum("rhd,khd->hrk", q_h, mem_k, preferred_element_type=f32) * inv_root
    mem_probs = jax.nn.softmax(mem_scores, axis=-1).astype(bf16)
    from_memory = jnp.einsum("hrk,khd->rhd", mem_probs, mem_v, preferred_element_type=f32)
    padded = jnp.pad(memory_rows, ((0, 3 * ncomp - seg), (0, 0)))
    windows = padded.reshape(ncomp, 3 * width)
    comp_new = mm(windows, comp_weight).astype(bf16)
    ckv_t = mm(comp_new, wkv_t).astype(bf16)
    comp_k = ckv_t[:, :cb].reshape(ncomp, hpt, head_dim)
    comp_v = ckv_t[:, cb:].reshape(ncomp, hpt, head_dim)
    comp_scores = jnp.einsum("rhd,khd->hrk", q_h, comp_k, preferred_element_type=f32) * inv_root
    comp_probs = jax.nn.softmax(comp_scores, axis=-1)
    comp_low = comp_probs.astype(bf16)
    from_comp = jnp.einsum("hrk,khd->rhd", comp_low, comp_v, preferred_element_type=f32)
    grad_fc = ((from_comp - from_memory) * mask_all[:, :, None]).astype(bf16)
    grad_cw = jnp.einsum("rhd,khd->hrk", grad_fc, comp_v, preferred_element_type=f32)
    grad_cs = softmax_grad(comp_probs, grad_cw)
    grad_ck = (
        jnp.einsum("hrk,rhd->khd", grad_cs, q_h, preferred_element_type=f32) * inv_root
    ).astype(bf16)
    grad_cv = jnp.einsum("hrk,rhd->khd", comp_low, grad_fc, preferred_element_type=f32).astype(bf16)
    grad_ckv = jnp.concatenate(
        [grad_ck.reshape(ncomp, cb), grad_cv.reshape(ncomp, cb)], axis=1
    )
    grad_comp_part = mm_nt(grad_ckv, wkv_t)
    grad_comp_t = lax.psum_scatter(grad_comp_part, "tier", scatter_dimension=1, tiled=True)
    grad_comp_t = grad_comp_t.astype(bf16)

    full_comp = jnp.concatenate([comp_rows[ncomp:], comp_new[:ncomp]], axis=0)
    new_compressed = lax.dynamic_slice_in_dim(full_comp, tier_pos * row_count, row_count, axis=0)

    hidden_f = hidden_own.astype(f32)
    residual = hidden_f + mm(attended, attn_out_weight)
    normed, norm_pull = jax.vjp(layer_norm, residual, norm_gain)
    normed_low = normed.astype(bf16)
    pre_act = mm(normed_low, ffn_in_weight)
    act_value, gelu_pull = jax.vjp(gelu_tanh, pre_act)
    activation = act_value.astype(bf16)
    ffn_result = mm(activation, ffn_out_weight)
    output = ((residual + ffn_result) * mask_own).astype(bf16)

    grad_rows = cotangent[0].astype(f32) * mask_own
    grad_low = grad_rows.astype(bf16)
    grad_act = mm_nt(grad_low, ffn_out_weight)
    grad_pre = gelu_pull(grad_act)[0].astype(bf16)
    grad_normed = mm_nt(grad_pre, ffn_in_weight)
    grad_resid_norm, part_gain = norm_pull(grad_normed)
    grad_resid = grad_rows + grad_resid_norm
    grad_att = grad_resid.astype(bf16)
    grad_attended = mm_nt(grad_att, attn_out_weight).astype(bf16)
    back_t = lax.all_to_all(jnp.stack([grad_attended, grad_att], axis=0), "tier", 2, 1, tiled=True)
    grad_attended_t = back_t[0]
    grad_att_t = back_t[1]

    fwd_seq = lax.all_gather(jnp.stack([normed_low, attended], axis=0), "tier", axis=1, tiled=True)
    normed_seq = fwd_seq[0]
    attended_seq = fwd_seq[1]
    grad_seq = (cot_seq.astype(f32) * mask_all).astype(bf16)
    pre_seq = mm(normed_seq, ffn_in_weight)
    act_seq = gelu_tanh(pre_seq).astype(bf16)
    fcol0 = tier_pos * ffb
    pre_seq_t = lax.dynamic_slice_in_dim(pre_seq, fcol0, ffb, axis=1)
    wfo_t = lax.dynamic_slice_in_dim(ffn_out_weight, fcol0, ffb, axis=0)
    grad_act_seq_t = mm_nt(grad_seq, wfo_t)
    _, gelu_pull_seq = jax.vjp(gelu_tanh, pre_seq_t)
    grad_pre_seq_t = gelu_pull_seq(grad_act_seq_t)[0].astype(bf16)
    grad_seq_t = lax.dynamic_slice_in_dim(grad_seq, col0, cb, axis=1)
    fused = all((m // seqs) % 128 == 0 for m in (width, ff, 3 * width))
    if not fused:
        part_comp = mm_tn(windows, grad_comp_t)
        part_ffn_in = mm_tn(normed_seq, grad_pre_seq_t)
        part_ffn_out = mm_tn(act_seq, grad_seq_t)
        part_attn_out = mm_tn(attended_seq, grad_att_t)
        early_parts = (part_attn_out, part_ffn_in, part_ffn_out, part_comp)
        early_parts = tuple(p.astype(bf16) for p in early_parts)
        early_parts, grad_attended_t = lax.optimization_barrier((early_parts, grad_attended_t))

    grad_att_h = grad_attended_t.reshape(seg, hpt, head_dim)
    grad_probs = jnp.einsum("rhd,khd->hrk", grad_att_h, v_h, preferred_element_type=f32)
    grad_scores = softmax_grad(probs, grad_probs)
    part_slope = -jnp.einsum("hrk,rk->h", grad_scores.astype(f32), distance)
    grad_q = (
        jnp.einsum("hrk,khd->rhd", grad_scores, k_h, preferred_element_type=f32) * inv_root
    ).reshape(seg, cb).astype(bf16)
    grad_k = (
        jnp.einsum("hrk,rhd->khd", grad_scores, q_h, preferred_element_type=f32) * inv_root
    ).reshape(keys_n, cb).astype(bf16)
    grad_v = jnp.einsum("hrk,rhd->khd", probs_low, grad_att_h, preferred_element_type=f32)
    grad_v = grad_v.reshape(keys_n, cb).astype(bf16)
    if not fused:
        part_query = mm_tn(hidden_seq, grad_q)
        part_key = mm_tn(context, grad_k)
        part_value = mm_tn(context, grad_v)
        late_parts = (part_query, part_key, part_value)

    seg_grads = jnp.stack([grad_q, grad_k[2 * seg :], grad_v[2 * seg :]], axis=0)
    own_grads = lax.all_to_all(seg_grads, "tier", 1, 2, tiled=True)
    grad_hidden = grad_resid + mm_nt(own_grads[0], query_weight)
    grad_hidden = grad_hidden + mm_nt(own_grads[1], key_weight)
    grad_hidden = grad_hidden + mm_nt(own_grads[2], value_weight)
    grad_input = grad_hidden * mask_own

    slope_full = lax.dynamic_update_slice_in_dim(jnp.zeros((width,), f32), part_slope, tier_pos * hpt, 0)
    small = jnp.zeros((8, width), f32).at[0].set(part_gain).at[1].set(slope_full)
    if fused:
        comp_pad = (-ncomp) % 16
        factors = (
            hidden_seq, grad_q, context, grad_k, grad_v, attended_seq, grad_att_t,
            normed_seq, grad_pre_seq_t, act_seq, grad_seq_t,
            jnp.pad(windows, ((0, comp_pad), (0, 0))), jnp.pad(grad_comp_t, ((0, comp_pad), (0, 0))),
        )
        plan = ((0, 1), (2, 3), (2, 4), (5, 6), (7, 8), (9, 10), (11, 12))
        *outs, small_total = ring_matmul_reduce(factors, plan, small, seqs, tiers)
    else:
        late_parts = tuple(p.astype(bf16) for p in late_parts)
        *outs, small_total = ring_reduce_scatter(late_parts + early_parts, small, seqs, tiers)
    gain_total = small_total[0]
    slope_total = small_total[1, :heads]
    return (
        output[None],
        grad_input[None],
        hidden_own[None],
        new_compressed[None],
        outs[0],
        outs[1],
        outs[2],
        outs[3],
        outs[4],
        outs[5],
        outs[6],
        gain_total,
        slope_total,
    )


def solution(mesh):
    placed = (
        P("seq", "tier", None),
        P("seq", "tier", None),
        P("seq", "tier", None),
        P("seq"),
        P("seq"),
        P(),
        P(),
        P(),
        P(),
        P(),
        P(),
        P(),
        P(),
        P(),
        P("seq", "tier", None),
    )
    return jax.shard_map(
        per_device,
        mesh=mesh,
        in_specs=placed,
        out_specs=(
            P("seq", "tier", None),
            P("seq", "tier", None),
            P("seq", "tier", None),
            P("seq", "tier", None),
            P("seq", "tier"),
            P("seq", "tier"),
            P("seq", "tier"),
            P("seq", "tier"),
            P("seq", "tier"),
            P("seq", "tier"),
            P("seq", "tier"),
            P(),
            P(),
        ),
        check_vma=False,
    )
```

profile of v0, /device:TPU:0, one launch (start us, length us, event | category | flops | bytes accessed | tf_op | source)
XLA Modules:
  0.0 330.2 jit_solution(4795397226210986291)
XLA Ops:
  9.8 2.0 pad_maximum_fusion.2
  15.7 3.1 fusion.44
  18.8 24.5 %all-gather.4.cloned.1.call-done = bf16[3,512,1024]{2,1,0:T(8,128)(2,1)} async-done(((bf16[3,128,1024]{2,1,0:T(8,128)(2,1)}), bf16[3,512,1024]{2,1,0:T(8,128)(2,1)}) %all-gather.4.cloned.1.call-update) | async-done | bytes 3145744 | tf_op jit(solution)/shard_map/all_gather | solution.py:395
  43.3 2.9 slice_bitcast_fusion.3
  52.5 2.5 reshape.321
  55.0 4.5 %convolution_convert_fusion.2 = bf16[171,1024]{1,0:T(8,128)(2,1)S(1)} fusion(bf16[171,3072]{1,0:T(8,128)(2,1)} %reshape.321, bf16[3072,1024]{1,0:T(8,128)(2,1)} %param.32), kind=kOutput, calls=%fused_computation.56 | convolution fusion | flops 1076014080 | bytes 7692288 | tf_op jit(solution)/shard_map/dot_general | solution.py:34
  64.1 2.3 fusion.91
  66.4 3.0 fusion.46
  71.0 2.4 multiply_reduce_fusion.3
  75.3 2.6 fusion.73
  77.9 4.1 %fusion.152 = (f32[2,512]{1,0:T(2,128)S(1)}, f32[2,512,1536]{2,1,0:T(8,128)S(1)}) fusion(f32[512,1536]{1,0:T(8,128)} %get-tuple-element.80, f32[2]{0:T(128)S(1)} %dynamic_slice.27, bf16[512,2,128]{0,2,1:T(8,128)(2,1)S(1)} %bitcast.180, bf16[1536,2,128]{0,2,1:T(8,128)(2,1)S(1)} %bitcast.151, pred[512,1536]{1,0:T(8,128)(4,1)} %fusion.14), kind=kOutput, calls=%fused_computation.194 | convolution fusion | flops 410516480 | bytes 11276296 | tf_op jit(solution)/shard_map/rhd,khd->hrk/dot_general | solution.py:422
  86.9 3.4 %all-to-all-start = ((bf16[4,128,256]{2,1,0:T(8,128)(2,1)}), bf16[4,128,256]{2,1,0:T(8,128)(2,1)S(1)}, u32[]{:S(2)}, u32[]{:S(2)}) async-start(bf16[4,128,256]{2,1,0:T(8,128)(2,1)} %copy.130), calls=%async_computation | async-start | bytes 524288 | tf_op jit(solution)/shard_map/all_to_all | solution.py:430
  90.6 2.3 pad.18.refs_11_
  93.0 3.7 %all-to-all-done = bf16[4,128,256]{2,1,0:T(8,128)(2,1)S(1)} async-done(((bf16[4,128,256]{2,1,0:T(8,128)(2,1)}), bf16[4,128,256]{2,1,0:T(8,128)(2,1)S(1)}, u32[]{:S(2)}, u32[]{:S(2)}) %all-to-all-start) | async-done | bytes 262176 | tf_op jit(solution)/shard_map/all_to_all | solution.py:430
  99.4 6.1 %fusion.133 = f32[128,4096]{1,0:T(8,128)} fusion(bf16[1024,4096]{1,0:T(8,128)(2,1)} %param.28, f32[128,1024]{1,0:T(8,128)S(1)} %get-tuple-element.84, f32[1024]{0:T(1024)S(1)} %copy-done.28, f32[128]{0:T(128)S(1)} %fusion.108, f32[128]{0:T(128)S(1)} %broadcast_multiply_fusion), kind=kOutput, calls=%fused_computation.187 | convolution fusion | flops 1074266112 | bytes 11015168 | tf_op jit(solution)/shard_map/dot_general | solution.py:34
  105.4 13.7 %multiply_reduce_fusion.4 = (f32[1024]{0:T(1024)S(1)}, f32[128]{0:T(128)S(1)}, f32[128,1024]{1,0:T(8,128)}) fusion(f32[128,1024]{1,0:T(8,128)S(1)} %get-tuple-element.84, f32[128]{0:T(128)S(1)} %fusion.108, f32[128]{0:T(128)S(1)} %broadcast_multiply_fusion, f32[1024]{0:T(1024)S(1)} %copy-done.28, bf16[1024,4096]{1,0:T(8,128)(2,1)} %param.28, ...), kind=kOutput, calls=%fused_computation.117 | convolution fusion | flops 2159279104 | bytes 20195328 | tf_op jit(solution)/shard_map/dot_general | solution.py:42
  119.2 2.0 fusion.146
  125.1 3.6 %all-to-all-start.1 = ((bf16[2,128,1024]{1,0,2:T(2,128)(2,1)}), bf16[2,128,1024]{1,0,2:T(2,128)(2,1)S(1)}, u32[]{:S(2)}, u32[]{:S(2)}) async-start(bf16[2,128,1024]{1,0,2:T(2,128)(2,1)} %copy.132), calls=%async_computation.1 | async-start | bytes 1048576 | tf_op jit(solution)/shard_map/all_to_all | solution.py:483
  133.7 3.8 %all-to-all-done.1 = bf16[2,128,1024]{1,0,2:T(2,128)(2,1)S(1)} async-done(((bf16[2,128,1024]{1,0,2:T(2,128)(2,1)}), bf16[2,128,1024]{1,0,2:T(2,128)(2,1)S(1)}, u32[]{:S(2)}, u32[]{:S(2)}) %all-to-all-start.1) | async-done | bytes 524320 | tf_op jit(solution)/shard_map/all_to_all | solution.py:483
  138.9 4.3 %convolution_convert_fusion.1 = bf16[2,128,1536]{2,1,0:T(8,128)(2,1)S(1)} fusion(bf16[512,2,128]{0,2,1:T(8,128)(2,1)S(1)} %copy.136, f32[2,512,1536]{2,1,0:T(8,128)} %copy-done.2, f32[2,512]{1,0:T(2,128)S(1)} %log_add_fusion), kind=kOutput, calls=%fused_computation.30 | convolution fusion | flops 406192128 | bytes 7344128 | tf_op jit(solution)/shard_map/hrk,rhd->khd/dot_general | solution.py:520
  143.2 6.7 %multiply_reduce_fusion.1 = (f32[2,512]{1,0:T(2,128)S(1)}, f32[2,512,1536]{2,1,0:T(8,128)}) fusion(f32[2,512,1536]{2,1,0:T(8,128)} %copy-done.2, f32[2,512]{1,0:T(2,128)S(1)} %log_add_fusion, bf16[512,2,128]{0,2,1:T(8,128)(2,1)S(1)} %copy.136, bf16[1536,2,128]{0,2,1:T(8,128)(2,1)S(1)} %bitcast.154), kind=kOutput, calls=%fused_computation.13 | convolution fusion | flops 407370752 | bytes 13639680 | tf_op jit(solution)/shard_map/rhd,khd->hrk/dot_general | solution.py:511
  151.0 6.9 %multiply_reduce_fusion = (f32[2]{0:T(128)S(1)}, bf16[2,512,1536]{2,1,0:T(8,128)(2,1)S(1)}) fusion(f32[1536,512]{0,1:T(8,128)} %get-tuple-element.79, f32[2,512,1536]{2,1,0:T(8,128)} %get-tuple-element.87, f32[2,512]{1,0:T(2,128)S(1)} %get-tuple-element.86, f32[2,512,1536]{2,1,0:T(8,128)} %copy-done.2, f32[2,512]{1,0:T(2,128)S(1)} %log_add_fusion), kind=kLoop, calls=%fused_computation.11 | loop fusion | flops 11010046 | bytes 18882568 | tf_op jit(solution)/shard_map/hrk,rk->h/dot_general | solution.py:513
  160.7 3.0 fusion.42
  164.2 4.0 %pad_maximum_fusion.1 = bf16[3,512,256]{2,0,1:T(4,128)(2,1)} fusion(bf16[1,512,256]{2,0,1:T(2,128)(2,1)} %copy.139, bf16[1,512,256]{2,0,1:T(2,128)(2,1)} %copy.138, bf16[1,512,256]{2,0,1:T(2,128)(2,1)S(1)} %copy.137), kind=kLoop, calls=%fused_computation.89 | loop fusion | flops 2359296 | bytes 1572864 | tf_op jit(solution)/shard_map/stack | solution.py:528
  168.1 4.2 %all-to-all-start.2 = ((bf16[3,512,256]{2,0,1:T(4,128)(2,1)}), bf16[3,512,256]{2,0,1:T(4,128)(2,1)}, u32[]{:S(2)}, u32[]{:S(2)}) async-start(bf16[3,512,256]{2,0,1:T(4,128)(2,1)} %pad_maximum_fusion.1), calls=%async_computation.2 | async-start | bytes 2097152 | tf_op jit(solution)/shard_map/all_to_all | solution.py:529
  172.4 6.3 %fusion.48 = bf16[1,128,1024]{2,1,0:T(8,128)(2,1)} fusion(f32[128,1024]{1,0:T(8,128)S(1)} %get-tuple-element.84, bf16[4096,1024]{1,0:T(8,128)(2,1)} %param.29, f32[128,4096]{1,0:T(8,128)} %fusion.133, f32[128]{0:T(128)S(1)} %compare_convert_fusion), kind=kOutput, calls=%fused_computation.79 | convolution fusion | flops 1078853632 | bytes 11272704 | tf_op jit(solution)/shard_map/dot_general | solution.py:34
  182.3 4.6 %all-to-all-done.2 = bf16[3,512,256]{2,0,1:T(4,128)(2,1)} async-done(((bf16[3,512,256]{2,0,1:T(4,128)(2,1)}), bf16[3,512,256]{2,0,1:T(4,128)(2,1)}, u32[]{:S(2)}, u32[]{:S(2)}) %all-to-all-start.2) | async-done | bytes 786464 | tf_op jit(solution)/shard_map/all_to_all | solution.py:529
  188.9 2.6 convolution_add_fusion.2
  198.5 11.8 %fusion.9 = (bf16[512,4096]{1,0:T(8,128)(2,1)}, f32[512,4096]{1,0:T(8,128)S(1)}) fusion(bf16[1024,4096]{1,0:T(8,128)(2,1)} %param.28, bf16[2,512,1024]{2,1,0:T(8,128)(2,1)} %all-gather.6.cloned.1.call-done), kind=kOutput, calls=%fused_computation.10 | convolution fusion | flops 4313841664 | bytes 22020096 | tf_op jit(solution)/shard_map/dot_general | solution.py:34
  210.3 5.1 %fusion.29.refs_8_ = bf16[512,1024]{1,0:T(8,128)(2,1)} fusion(f32[512,4096]{1,0:T(8,128)S(1)} %get-tuple-element.89, s32[]{:T(128)S(6)} %select_n.39, bf16[512,1024]{1,0:T(8,128)(2,1)S(1)} %multiply_convert_fusion.1, bf16[4096,1024]{1,0:T(8,128)(2,1)} %param.29), kind=kOutput, calls=%fused_computation.44 | convolution fusion | flops 1084227584 | bytes 6292480 | tf_op jit(solution)/shard_map/dot_general | solution.py:42
  216.9 94.2 %shard_map.246 = (f32[128,256]{1,0:T(8,128)}, f32[128,256]{1,0:T(8,128)}, f32[128,256]{1,0:T(8,128)}, f32[128,256]{1,0:T(8,128)}, f32[128,1024]{1,0:T(8,128)}, /...) custom-call(bf16[512,1024]{1,0:T(8,128)(2,1)} %get-tuple-element.63.refs_0_, ...), custom_call_target="tpu_custom_call" | custom-call | tf_op jit(solution)/shard_map/pallas_call | solution.py:325
  320.0 1.9 copy.223
  (160 shorter events, 66.1 us)
Async XLA Ops:
  7.2 90.4 %copy-start = (bf16[1024,1024]{1,0:T(8,128)(2,1)S(1)}, bf16[1024,1024]{1,0:T(8,128)(2,1)}, u32[]{:S(2)}) copy-start(bf16[1024,1024]{1,0:T(8,128)(2,1)} %param.27) | copy-start | bytes 6291460
  7.2 5.4 %copy-start.30 = (f32[8]{0:T(128)S(1)}, f32[8]{0:T(128)}, u32[]{:S(2)}) copy-start(f32[8]{0:T(128)} %param.31) | copy-start | bytes 100
  7.2 36.0 %all-gather.4.cloned.1.call-start = ((), (), s32[]{:S(2)}) async-start(), calls=%async_computation.4 | async-start | bytes 3932160 | tf_op jit(solution)/shard_map/all_gather | solution.py:395
  11.9 182.8 %reduce-scatter.2.cloned.1.call-start = ((), (), s32[]{:S(2)}) async-start(), calls=%async_computation.7 | async-start | bytes 901120 | tf_op jit(solution)/shard_map/reduce_scatter | solution.py:458
  14.0 32.2 %copy-start.18 = (bf16[1024,256]{1,0:T(8,128)(2,1)}, bf16[1024,256]{1,0:T(8,128)(2,1)S(1)}, u32[]{:S(2)}) copy-start(bf16[1024,256]{1,0:T(8,128)(2,1)S(1)} %get-tuple-element.94) | copy-start | bytes 1572868
  14.0 32.2 %copy-start.20 = (bf16[1024,256]{1,0:T(8,128)(2,1)}, bf16[1024,256]{1,0:T(8,128)(2,1)S(1)}, u32[]{:S(2)}) copy-start(bf16[1024,256]{1,0:T(8,128)(2,1)S(1)} %get-tuple-element.95) | copy-start | bytes 1572868
  43.3 2.9 copy-start.4
  51.4 26.5 %copy-start.16 = (bf16[512,256]{0,1:T(8,128)(2,1)}, bf16[512,256]{0,1:T(8,128)(2,1)S(1)}, u32[]{:S(2)}) copy-start(bf16[512,256]{0,1:T(8,128)(2,1)S(1)} %convolution_convert_fusion.5) | copy-start | bytes 786436
  55.0 4.5 %copy-start.19 = (bf16[1024,256]{1,0:T(8,128)(2,1)S(1)}, bf16[1024,256]{1,0:T(8,128)(2,1)}, u32[]{:S(2)}) copy-start(bf16[1024,256]{1,0:T(8,128)(2,1)} %copy-done.18) | copy-start | bytes 1572868
  55.0 4.5 %copy-start.21 = (bf16[1024,256]{1,0:T(8,128)(2,1)S(1)}, bf16[1024,256]{1,0:T(8,128)(2,1)}, u32[]{:S(2)}) copy-start(bf16[1024,256]{1,0:T(8,128)(2,1)} %copy-done.20) | copy-start | bytes 1572868
  61.1 8.3 %copy-start.29 = (bf16[171,2,128]{2,1,0:T(2,128)(2,1)}, bf16[171,2,128]{2,1,0:T(2,128)(2,1)S(1)}, u32[]{:S(2)}) copy-start(bf16[171,2,128]{2,1,0:T(2,128)(2,1)S(1)} %reshape.322) | copy-start | bytes 262660
  64.1 2.3 copy-start.26
  82.0 2.7 copy-start.2
  82.0 2.6 copy-start.5
  86.9 9.8 %all-to-all-start = ((bf16[4,128,256]{2,1,0:T(8,128)(2,1)}), bf16[4,128,256]{2,1,0:T(8,128)(2,1)S(1)}, u32[]{:S(2)}, u32[]{:S(2)}) async-start(bf16[4,128,256]{2,1,0:T(8,128)(2,1)} %copy.130), calls=%async_computation | async-start | bytes 524288 | tf_op jit(solution)/shard_map/all_to_all | solution.py:430
  90.3 106.0 %all-gather.8.cloned.1.call-start = ((), (), s32[]{:S(2)}) async-start(), calls=%async_computation.6 | async-start | bytes 1310720 | tf_op jit(solution)/shard_map/all_gather | solution.py:397
  93.0 6.4 %copy-start.28 = (f32[1024]{0:T(1024)S(1)}, f32[1024]{0:T(1024)}, u32[]{:S(2)}) copy-start(f32[1024]{0:T(1024)} %param.30) | copy-start | bytes 12292
  123.9 6.5 %copy-start.25 = (bf16[171,1024]{1,0:T(8,128)(2,1)S(1)}, bf16[171,1024]{1,0:T(8,128)(2,1)}, u32[]{:S(2)}) copy-start(bf16[171,1024]{1,0:T(8,128)(2,1)} %copy-done.24) | copy-start | bytes 1050628
  125.1 6.4 %copy-start.12 = (bf16[4,128,256]{2,1,0:T(8,128)(2,1)S(1)}, bf16[4,128,256]{2,1,0:T(8,128)(2,1)}, u32[]{:S(2)}) copy-start(bf16[4,128,256]{2,1,0:T(8,128)(2,1)} %copy-done.11) | copy-start | bytes 786436
  125.1 12.4 %all-to-all-start.1 = ((bf16[2,128,1024]{1,0,2:T(2,128)(2,1)}), bf16[2,128,1024]{1,0,2:T(2,128)(2,1)S(1)}, u32[]{:S(2)}, u32[]{:S(2)}) async-start(bf16[2,128,1024]{1,0,2:T(2,128)(2,1)} %copy.132), calls=%async_computation.1 | async-start | bytes 1048576 | tf_op jit(solution)/shard_map/all_to_all | solution.py:483
  128.7 69.8 %all-gather.6.cloned.1.call-start = ((), (), s32[]{:S(2)}) async-start(), calls=%async_computation.5 | async-start | bytes 2621440 | tf_op jit(solution)/shard_map/all_gather | solution.py:487
  138.9 4.3 %copy-start.6 = (bf16[1536,256]{0,1:T(8,128)(2,1)S(1)}, bf16[1536,256]{0,1:T(8,128)(2,1)}, u32[]{:S(2)}) copy-start(bf16[1536,256]{0,1:T(8,128)(2,1)} %get-tuple-element.70) | copy-start | bytes 2359300
  151.0 6.9 %copy-start.17 = (bf16[512,256]{0,1:T(8,128)(2,1)S(1)}, bf16[512,256]{0,1:T(8,128)(2,1)}, u32[]{:S(2)}) copy-start(bf16[512,256]{0,1:T(8,128)(2,1)} %copy-done.16) | copy-start | bytes 786436
  168.1 18.8 %all-to-all-start.2 = ((bf16[3,512,256]{2,0,1:T(4,128)(2,1)}), bf16[3,512,256]{2,0,1:T(4,128)(2,1)}, u32[]{:S(2)}, u32[]{:S(2)}) async-start(bf16[3,512,256]{2,0,1:T(4,128)(2,1)} %pad_maximum_fusion.1), calls=%async_computation.2 | async-start | bytes 2097152 | tf_op jit(solution)/shard_map/all_to_all | solution.py:529
  182.3 6.4 %copy-start.27 = (f32[8,1024]{1,0:T(8,128)}, f32[8,1024]{1,0:T(8,128)S(1)}, u32[]{:S(2)}) copy-start(f32[8,1024]{1,0:T(8,128)S(1)} %scatter.9.refs_13_) | copy-start | bytes 98308
  182.3 6.5 %copy-start.8 = (f32[128,1024]{1,0:T(8,128)S(1)}, f32[128,1024]{1,0:T(8,128)}, u32[]{:S(2)}) copy-start(f32[128,1024]{1,0:T(8,128)} %copy-done.7) | copy-start | bytes 1572868
  182.3 6.5 %copy-start.13 = (bf16[1,128,1024]{2,1,0:T(8,128)(2,1)S(1)}, bf16[1,128,1024]{2,1,0:T(8,128)(2,1)}, u32[]{:S(2)}) copy-start(bf16[1,128,1024]{2,1,0:T(8,128)(2,1)} %param.33) | copy-start | bytes 786436
  188.9 2.6 copy-start.10
  210.3 5.1 %copy-start.14 = (bf16[2,512,1024]{2,1,0:T(8,128)(2,1)S(1)}, bf16[2,512,1024]{2,1,0:T(8,128)(2,1)}, u32[]{:S(2)}) copy-start(bf16[2,512,1024]{2,1,0:T(8,128)(2,1)} %all-gather.6.cloned.1.call-done) | copy-start | bytes 6291460
  216.9 106.5 %copy-start.1 = (bf16[1024,1024]{1,0:T(8,128)(2,1)S(1)}, bf16[1024,1024]{1,0:T(8,128)(2,1)}, u32[]{:S(2)}) copy-start(bf16[1024,1024]{1,0:T(8,128)(2,1)} %param.27) | copy-start | bytes 6291460
  311.1 10.8 %copy-start.22 = (f32[512,256]{1,0:T(8,128)S(1)}, f32[512,256]{1,0:T(8,128)}, u32[]{:S(2)}) copy-start(f32[512,256]{1,0:T(8,128)} %get-tuple-element.120) | copy-start | bytes 1572868
  311.1 11.6 %copy-start.23 = (f32[384,256]{1,0:T(8,128)S(1)}, f32[384,256]{1,0:T(8,128)}, u32[]{:S(2)}) copy-start(f32[384,256]{1,0:T(8,128)} %get-tuple-element.121) | copy-start | bytes 1179652
  (6 other events, 6.3 us)
Sparse Core Ops, SparseCore 0:
  12.0 31.2 all-gather.3
  78.0 23.1 reduce-scatter.1
  102.8 16.7 all-gather.7
  133.8 23.9 all-gather.5
where the time goes:
time: 335 us; the launch traced here: 330 us
  matrix products  95 us (28%)
  Pallas kernels  94.2 us (28%)
  local copies, waits for them, and re-layouts  47.7 us (14%)
  waiting for transfers between devices  36.6 us (11%)
  other arithmetic  28.4 us (8%)
  between operations  16.1 us (5%)
  starting transfers between devices  12 us (4%)
    pallas_call x1, Pallas kernels, ring_matmul_reduce(): pl.pallas_call(functools.partial(ring_mm_kernel, seqs, tiers, tuple(plan)...  94.2 us
    dot_general x8, matrix products, mm(): return jnp.dot(left, right, preferred_element_type=f32)  34 us
    dot_general x7, matrix products, mm_nt(): lax.dot_general(left, right, (((1,), (1,)), ((), ())), preferred_element_...  27.3 us
    all_gather x1, waiting for transfers between devices, per_device(): raw_seq = lax.all_gather(raw_local, 'tier', axis=1, tiled=True)  24.5 us
    unnamed x73, local copies, waits for them, and re-layouts  15.2 us
    dot_general x1, other arithmetic, per_device(): part_slope = -jnp.einsum('hrk,rk->h', grad_scores.astype(f32), distance)  6.93 us
    dot_general x1, matrix products, per_device(): jnp.einsum('rhd,khd->hrk', grad_att_h, v_h, preferred_element_type=f32)  6.74 us
  transfers between devices with their start and end apart: 7, of which 4 were waited for; matrix products, arithmetic and copies ran while one was open for 30% of the time, Pallas kernels for 0%

commit v1 on v0

--- a/solution.py
+++ b/solution.py
@@ -464,17 +464,17 @@
     hidden_f = hidden_own.astype(f32)
     residual = hidden_f + mm(attended, attn_out_weight)
     normed, norm_pull = jax.vjp(layer_norm, residual, norm_gain)
-    normed_low = normed.astype(bf16)
+    normed_low = lax.optimization_barrier(normed.astype(bf16))
     pre_act = mm(normed_low, ffn_in_weight)
     act_value, gelu_pull = jax.vjp(gelu_tanh, pre_act)
-    activation = act_value.astype(bf16)
+    activation = lax.optimization_barrier(act_value.astype(bf16))
     ffn_result = mm(activation, ffn_out_weight)
     output = ((residual + ffn_result) * mask_own).astype(bf16)
 
     grad_rows = cotangent[0].astype(f32) * mask_own
     grad_low = grad_rows.astype(bf16)
     grad_act = mm_nt(grad_low, ffn_out_weight)
-    grad_pre = gelu_pull(grad_act)[0].astype(bf16)
+    grad_pre = lax.optimization_barrier(gelu_pull(grad_act)[0].astype(bf16))
     grad_normed = mm_nt(grad_pre, ffn_in_weight)
     grad_resid_norm, part_gain = norm_pull(grad_normed)
     grad_resid = grad_rows + grad_resid_norm

time: 335 us -> 321 us (0.958)
  matrix products: 95 us -> 84.7 us
  other arithmetic: 28.4 us -> 23.8 us
    dot_general x7 -> x8, matrix products: 27.3 us -> 20.1 us  [mm_nt(): lax.dot_general(left, right, (((1,), (1,)), ((), ())), preferred_element_...]
    unnamed x73 -> x89, local copies, waits for them, and re-layouts: 15.2 us -> 14.2 us
  transfers between devices with their start and end apart: 7 -> 7, of which waited for: 4 -> 4; matrix products, arithmetic and copies ran while one was open for 30% -> 26% of each run, Pallas kernels for 0% -> 0%
where the time goes in v1:
time: 321 us; the launch traced here: 316 us
  Pallas kernels  94.1 us (29%)
  matrix products  84.7 us (26%)
  local copies, waits for them, and re-layouts  46.7 us (15%)
  waiting for transfers between devices  38.1 us (12%)
  other arithmetic  23.8 us (7%)
  between operations  16.2 us (5%)
  starting transfers between devices  12 us (4%)
    pallas_call x1, Pallas kernels, ring_matmul_reduce(): pl.pallas_call(functools.partial(ring_mm_kernel, seqs, tiers, tuple(plan)...  94.1 us
    dot_general x8, matrix products, mm(): return jnp.dot(left, right, preferred_element_type=f32)  33.8 us
    all_gather x1, waiting for transfers between devices, per_device(): raw_seq = lax.all_gather(raw_local, 'tier', axis=1, tiled=True)  24.5 us
    dot_general x8, matrix products, mm_nt(): lax.dot_general(left, right, (((1,), (1,)), ((), ())), preferred_element_...  20.1 us
    unnamed x89, local copies, waits for them, and re-layouts  14.2 us
  transfers between devices with their start and end apart: 7, of which 4 were waited for; matrix products, arithmetic and copies ran while one was open for 26% of the time, Pallas kernels for 0%

profile of v1, /device:TPU:0, one launch (start us, length us, event | category | flops | bytes accessed | tf_op | source)
XLA Modules:
  0.0 315.7 jit_solution(16548156808201822372)
XLA Ops:
  9.8 2.0 pad_maximum_fusion.2
  15.7 3.1 fusion.44
  18.8 24.5 %all-gather.4.cloned.1.call-done = bf16[3,512,1024]{2,1,0:T(8,128)(2,1)} async-done(((bf16[3,128,1024]{2,1,0:T(8,128)(2,1)}), bf16[3,512,1024]{2,1,0:T(8,128)(2,1)}) %all-gather.4.cloned.1.call-update) | async-done | bytes 3145744 | tf_op jit(solution)/shard_map/all_gather | solution.py:395
  43.3 2.9 slice_bitcast_fusion.3
  52.4 2.5 reshape.321
  54.9 4.5 %convolution_convert_fusion.2 = bf16[171,1024]{1,0:T(8,128)(2,1)S(1)} fusion(bf16[171,3072]{1,0:T(8,128)(2,1)} %reshape.321, bf16[3072,1024]{1,0:T(8,128)(2,1)} %param.32), kind=kOutput, calls=%fused_computation.56 | convolution fusion | flops 1076014080 | bytes 7692288 | tf_op jit(solution)/shard_map/dot_general | solution.py:34
  64.1 2.3 fusion.76
  66.3 3.0 fusion.46
  71.0 2.4 multiply_reduce_fusion.3
  75.2 2.6 fusion.61
  77.8 4.1 %fusion.124 = (f32[2,512]{1,0:T(2,128)S(1)}, f32[2,512,1536]{2,1,0:T(8,128)S(1)}) fusion(f32[512,1536]{1,0:T(8,128)} %get-tuple-element.79, f32[2]{0:T(128)S(1)} %dynamic_slice.27, bf16[512,2,128]{0,2,1:T(8,128)(2,1)S(1)} %bitcast.186, bf16[1536,2,128]{0,2,1:T(8,128)(2,1)S(1)} %bitcast.156, pred[512,1536]{1,0:T(8,128)(4,1)} %fusion.14), kind=kOutput, calls=%fused_computation.171 | convolution fusion | flops 410516480 | bytes 11276296 | tf_op jit(solution)/shard_map/rhd,khd->hrk/dot_general | solution.py:422
  86.9 3.4 %all-to-all-start = ((bf16[4,128,256]{2,1,0:T(8,128)(2,1)}), bf16[4,128,256]{2,1,0:T(8,128)(2,1)S(1)}, u32[]{:S(2)}, u32[]{:S(2)}) async-start(bf16[4,128,256]{2,1,0:T(8,128)(2,1)} %copy.130), calls=%async_computation | async-start | bytes 524288 | tf_op jit(solution)/shard_map/all_to_all | solution.py:430
  90.5 2.3 pad.18.refs_11_
  92.9 3.5 %all-to-all-done = bf16[4,128,256]{2,1,0:T(8,128)(2,1)S(1)} async-done(((bf16[4,128,256]{2,1,0:T(8,128)(2,1)}), bf16[4,128,256]{2,1,0:T(8,128)(2,1)S(1)}, u32[]{:S(2)}, u32[]{:S(2)}) %all-to-all-start) | async-done | bytes 262176 | tf_op jit(solution)/shard_map/all_to_all | solution.py:430
  99.5 6.3 %multiply_convert_fusion.2 = (bf16[128,4096]{1,0:T(8,128)(2,1)}, f32[128,4096]{1,0:T(8,128)S(1)}) fusion(bf16[128,1024]{1,0:T(8,128)(2,1)S(1)} %multiply_convert_fusion.4, bf16[1024,4096]{1,0:T(8,128)(2,1)} %param.28), kind=kOutput, calls=%fused_computation.50 | convolution fusion | flops 1078460416 | bytes 11796480 | tf_op jit(solution)/shard_map/dot_general | solution.py:34
  105.8 3.6 %fusion.22 = bf16[128,4096]{1,0:T(8,128)(2,1)S(1)} fusion(f32[128,4096]{1,0:T(8,128)S(1)} %get-tuple-element.85, bf16[4096,1024]{1,0:T(8,128)(2,1)S(1)} %bitcast.151, f32[128]{0:T(128)S(1)} %compare_convert_fusion, bf16[1,128,1024]{2,1,0:T(8,128)(2,1)S(1)} %copy-done.13), kind=kOutput, calls=%fused_computation.37 | convolution fusion | flops 1084620800 | bytes 11796992 | tf_op jit(solution)/shard_map/dot_general | solution.py:42
  109.5 3.0 multiply_reduce_fusion.4
  115.7 3.6 %all-to-all-start.1 = ((bf16[2,128,1024]{1,0,2:T(2,128)(2,1)}), bf16[2,128,1024]{1,0,2:T(2,128)(2,1)S(1)}, u32[]{:S(2)}, u32[]{:S(2)}) async-start(bf16[2,128,1024]{1,0,2:T(2,128)(2,1)} %copy.132), calls=%async_computation.1 | async-start | bytes 1048576 | tf_op jit(solution)/shard_map/all_to_all | solution.py:483
  123.3 4.8 %all-to-all-done.1 = bf16[2,128,1024]{1,0,2:T(2,128)(2,1)S(1)} async-done(((bf16[2,128,1024]{1,0,2:T(2,128)(2,1)}), bf16[2,128,1024]{1,0,2:T(2,128)(2,1)S(1)}, u32[]{:S(2)}, u32[]{:S(2)}) %all-to-all-start.1) | async-done | bytes 524320 | tf_op jit(solution)/shard_map/all_to_all | solution.py:483
  129.5 4.7 %multiply_reduce_fusion.1 = (f32[2,512]{1,0:T(2,128)S(1)}, f32[2,512,1536]{2,1,0:T(8,128)S(1)}) fusion(f32[2,512,1536]{2,1,0:T(8,128)} %copy-done.2, f32[2,512]{1,0:T(2,128)S(1)} %log_add_fusion, bf16[512,2,128]{0,2,1:T(8,128)(2,1)S(1)} %copy.136, bf16[1536,2,128]{0,2,1:T(8,128)(2,1)S(1)} %bitcast.159), kind=kOutput, calls=%fused_computation.13 | convolution fusion | flops 407370752 | bytes 13639680 | tf_op jit(solution)/shard_map/rhd,khd->hrk/dot_general | solution.py:511
  134.3 5.9 %multiply_reduce_fusion = (f32[2]{0:T(128)S(1)}, bf16[2,512,1536]{2,1,0:T(8,128)(2,1)}) fusion(f32[1536,512]{0,1:T(8,128)S(1)} %copy-done.3, f32[2,512,1536]{2,1,0:T(8,128)S(1)} %get-tuple-element.88, f32[2,512]{1,0:T(2,128)S(1)} %get-tuple-element.87, f32[2,512,1536]{2,1,0:T(8,128)} %copy-done.2, f32[2,512]{1,0:T(2,128)S(1)} %log_add_fusion), kind=kLoop, calls=%fused_computation.11 | loop fusion | flops 11010046 | bytes 18882568 | tf_op jit(solution)/shard_map/hrk,rk->h/dot_general | solution.py:513
  142.6 2.5 fusion.15
  146.2 3.0 fusion.42
  149.7 4.0 %pad_maximum_fusion.1 = bf16[3,512,256]{2,0,1:T(4,128)(2,1)} fusion(bf16[1,512,256]{2,0,1:T(2,128)(2,1)} %copy.139, bf16[1,512,256]{2,0,1:T(2,128)(2,1)} %copy.138, bf16[1,512,256]{2,0,1:T(2,128)(2,1)S(1)} %copy.137), kind=kLoop, calls=%fused_computation.88 | loop fusion | flops 2359296 | bytes 1572864 | tf_op jit(solution)/shard_map/stack | solution.py:528
  153.7 4.2 %all-to-all-start.2 = ((bf16[3,512,256]{2,0,1:T(4,128)(2,1)}), bf16[3,512,256]{2,0,1:T(4,128)(2,1)}, u32[]{:S(2)}, u32[]{:S(2)}) async-start(bf16[3,512,256]{2,0,1:T(4,128)(2,1)} %pad_maximum_fusion.1), calls=%async_computation.2 | async-start | bytes 2097152 | tf_op jit(solution)/shard_map/all_to_all | solution.py:529
  157.9 5.7 %fusion.48 = bf16[1,128,1024]{2,1,0:T(8,128)(2,1)} fusion(f32[128,1024]{1,0:T(8,128)S(1)} %get-tuple-element.83, bf16[128,4096]{1,0:T(8,128)(2,1)} %get-tuple-element.84, bf16[4096,1024]{1,0:T(8,128)(2,1)} %param.29, f32[128]{0:T(128)S(1)} %compare_convert_fusion), kind=kOutput, calls=%fused_computation.79 | convolution fusion | flops 1074135040 | bytes 10224128 | tf_op jit(solution)/shard_map/dot_general | solution.py:34
  167.2 5.2 %all-to-all-done.2 = bf16[3,512,256]{2,0,1:T(4,128)(2,1)} async-done(((bf16[3,512,256]{2,0,1:T(4,128)(2,1)}), bf16[3,512,256]{2,0,1:T(4,128)(2,1)}, u32[]{:S(2)}, u32[]{:S(2)}) %all-to-all-start.2) | async-done | bytes 786464 | tf_op jit(solution)/shard_map/all_to_all | solution.py:529
  174.4 2.6 convolution_add_fusion.2
  184.0 11.8 %fusion.9 = (bf16[512,4096]{1,0:T(8,128)(2,1)}, f32[512,4096]{1,0:T(8,128)S(1)}) fusion(bf16[1024,4096]{1,0:T(8,128)(2,1)} %param.28, bf16[2,512,1024]{2,1,0:T(8,128)(2,1)} %all-gather.6.cloned.1.call-done), kind=kOutput, calls=%fused_computation.10 | convolution fusion | flops 4313841664 | bytes 22020096 | tf_op jit(solution)/shard_map/dot_general | solution.py:34
  195.8 5.1 %fusion.29.refs_8_ = bf16[512,1024]{1,0:T(8,128)(2,1)} fusion(f32[512,4096]{1,0:T(8,128)S(1)} %get-tuple-element.90, s32[]{:T(128)S(6)} %select_n.39, bf16[512,1024]{1,0:T(8,128)(2,1)S(1)} %multiply_convert_fusion.1, bf16[4096,1024]{1,0:T(8,128)(2,1)} %param.29), kind=kOutput, calls=%fused_computation.44 | convolution fusion | flops 1084227584 | bytes 6292480 | tf_op jit(solution)/shard_map/dot_general | solution.py:42
  202.5 94.1 %shard_map.246 = (f32[128,256]{1,0:T(8,128)}, f32[128,256]{1,0:T(8,128)}, f32[128,256]{1,0:T(8,128)}, f32[128,256]{1,0:T(8,128)}, f32[128,1024]{1,0:T(8,128)}, /...) custom-call(bf16[512,1024]{1,0:T(8,128)(2,1)} %get-tuple-element.63.refs_0_, ...), custom_call_target="tpu_custom_call" | custom-call | tf_op jit(solution)/shard_map/pallas_call | solution.py:325
  305.5 1.9 copy.223
  (181 shorter events, 64.4 us)
Async XLA Ops:
  7.2 90.1 %copy-start = (bf16[1024,1024]{1,0:T(8,128)(2,1)S(1)}, bf16[1024,1024]{1,0:T(8,128)(2,1)}, u32[]{:S(2)}) copy-start(bf16[1024,1024]{1,0:T(8,128)(2,1)} %param.27) | copy-start | bytes 6291460
  7.2 5.4 %copy-start.32 = (f32[8]{0:T(128)S(1)}, f32[8]{0:T(128)}, u32[]{:S(2)}) copy-start(f32[8]{0:T(128)} %param.31) | copy-start | bytes 100
  7.2 36.0 %all-gather.4.cloned.1.call-start = ((), (), s32[]{:S(2)}) async-start(), calls=%async_computation.4 | async-start | bytes 3932160 | tf_op jit(solution)/shard_map/all_gather | solution.py:395
  11.9 168.4 %reduce-scatter.2.cloned.1.call-start = ((), (), s32[]{:S(2)}) async-start(), calls=%async_computation.7 | async-start | bytes 901120 | tf_op jit(solution)/shard_map/reduce_scatter | solution.py:458
  14.0 32.2 %copy-start.21 = (bf16[1024,256]{1,0:T(8,128)(2,1)}, bf16[1024,256]{1,0:T(8,128)(2,1)S(1)}, u32[]{:S(2)}) copy-start(bf16[1024,256]{1,0:T(8,128)(2,1)S(1)} %get-tuple-element.95) | copy-start | bytes 1572868
  14.0 32.1 %copy-start.23 = (bf16[1024,256]{1,0:T(8,128)(2,1)}, bf16[1024,256]{1,0:T(8,128)(2,1)S(1)}, u32[]{:S(2)}) copy-start(bf16[1024,256]{1,0:T(8,128)(2,1)S(1)} %get-tuple-element.96) | copy-start | bytes 1572868
  51.3 26.5 %copy-start.19 = (bf16[512,256]{0,1:T(8,128)(2,1)}, bf16[512,256]{0,1:T(8,128)(2,1)S(1)}, u32[]{:S(2)}) copy-start(bf16[512,256]{0,1:T(8,128)(2,1)S(1)} %convolution_convert_fusion.5) | copy-start | bytes 786436
  54.9 4.5 %copy-start.24 = (bf16[1024,256]{1,0:T(8,128)(2,1)S(1)}, bf16[1024,256]{1,0:T(8,128)(2,1)}, u32[]{:S(2)}) copy-start(bf16[1024,256]{1,0:T(8,128)(2,1)} %copy-done.23) | copy-start | bytes 1572868
  61.0 8.3 %copy-start.30 = (bf16[171,2,128]{2,1,0:T(2,128)(2,1)}, bf16[171,2,128]{2,1,0:T(2,128)(2,1)S(1)}, u32[]{:S(2)}) copy-start(bf16[171,2,128]{2,1,0:T(2,128)(2,1)S(1)} %reshape.322) | copy-start | bytes 262660
  86.9 9.6 %all-to-all-start = ((bf16[4,128,256]{2,1,0:T(8,128)(2,1)}), bf16[4,128,256]{2,1,0:T(8,128)(2,1)S(1)}, u32[]{:S(2)}, u32[]{:S(2)}) async-start(bf16[4,128,256]{2,1,0:T(8,128)(2,1)} %copy.130), calls=%async_computation | async-start | bytes 524288 | tf_op jit(solution)/shard_map/all_to_all | solution.py:430
  90.3 91.5 %all-gather.8.cloned.1.call-start = ((), (), s32[]{:S(2)}) async-start(), calls=%async_computation.6 | async-start | bytes 1310720 | tf_op jit(solution)/shard_map/all_gather | solution.py:397
  92.9 6.4 %copy-start.31 = (f32[1024]{0:T(1024)S(1)}, f32[1024]{0:T(1024)}, u32[]{:S(2)}) copy-start(f32[1024]{0:T(1024)} %param.30) | copy-start | bytes 12292
  97.3 8.5 %slice-start.2 = ((s8[8388608]{0:T(1024)(128)(4,1)}), s8[4194304]{0:T(1024)(128)(4,1)S(1)}, s32[]{:S(2)}) async-start(s8[8388608]{0:T(1024)(128)(4,1)} %bitcast.150), calls=%async_computation.10 | async-start | bytes 8388608
  99.4 6.4 %copy-start.17 = (bf16[128,1024]{1,0:T(8,128)(2,1)}, bf16[128,1024]{1,0:T(8,128)(2,1)S(1)}, u32[]{:S(2)}) copy-start(bf16[128,1024]{1,0:T(8,128)(2,1)S(1)} %multiply_convert_fusion.4) | copy-start | bytes 786436
  99.4 6.4 %slice-start.3 = ((s8[8388608]{0:T(1024)(128)(4,1)}), s8[4194304]{0:T(1024)(128)(4,1)S(1)}, s32[]{:S(2)}) async-start(s8[8388608]{0:T(1024)(128)(4,1)} %bitcast.150), calls=%async_computation.11 | async-start | bytes 8388608
  99.4 6.4 %copy-start.13 = (bf16[1,128,1024]{2,1,0:T(8,128)(2,1)S(1)}, bf16[1,128,1024]{2,1,0:T(8,128)(2,1)}, u32[]{:S(2)}) copy-start(bf16[1,128,1024]{2,1,0:T(8,128)(2,1)} %param.33) | copy-start | bytes 786436
  99.5 10.0 %slice-start.4 = ((s8[8388608]{0:T(1024)(128)(4,1)}), s8[4194304]{0:T(1024)(128)(4,1)S(1)}, s32[]{:S(2)}) async-start(s8[8388608]{0:T(1024)(128)(4,1)} %bitcast.154), calls=%async_computation.12 | async-start | bytes 8388608
  115.7 6.4 %copy-start.12 = (bf16[4,128,256]{2,1,0:T(8,128)(2,1)S(1)}, bf16[4,128,256]{2,1,0:T(8,128)(2,1)}, u32[]{:S(2)}) copy-start(bf16[4,128,256]{2,1,0:T(8,128)(2,1)} %copy-done.11) | copy-start | bytes 786436
  115.7 12.4 %all-to-all-start.1 = ((bf16[2,128,1024]{1,0,2:T(2,128)(2,1)}), bf16[2,128,1024]{1,0,2:T(2,128)(2,1)S(1)}, u32[]{:S(2)}, u32[]{:S(2)}) async-start(bf16[2,128,1024]{1,0,2:T(2,128)(2,1)} %copy.132), calls=%async_computation.1 | async-start | bytes 1048576 | tf_op jit(solution)/shard_map/all_to_all | solution.py:483
  119.3 64.7 %all-gather.6.cloned.1.call-start = ((), (), s32[]{:S(2)}) async-start(), calls=%async_computation.5 | async-start | bytes 2621440 | tf_op jit(solution)/shard_map/all_gather | solution.py:487
  123.3 6.2 %copy-start.6 = (bf16[1536,256]{0,1:T(8,128)(2,1)S(1)}, bf16[1536,256]{0,1:T(8,128)(2,1)}, u32[]{:S(2)}) copy-start(bf16[1536,256]{0,1:T(8,128)(2,1)} %get-tuple-element.70) | copy-start | bytes 2359300
  129.5 4.8 %copy-start.3 = (f32[1536,512]{0,1:T(8,128)S(1)}, f32[1536,512]{0,1:T(8,128)}, u32[]{:S(2)}) copy-start(f32[1536,512]{0,1:T(8,128)} %get-tuple-element.78) | copy-start | bytes 9437188
  129.5 10.6 %slice-start = ((s8[6291456]{0:T(1024)(128)(4,1)}), s8[4194304]{0:T(1024)(128)(4,1)S(1)}, s32[]{:S(2)}) async-start(s8[6291456]{0:T(1024)(128)(4,1)} %bitcast.148), calls=%async_computation.8 | async-start | bytes 8388608
  134.3 5.9 %slice-start.1 = ((s8[6291456]{0:T(1024)(128)(4,1)}), s8[2097152]{0:T(1024)(128)(4,1)S(1)}, s32[]{:S(2)}) async-start(s8[6291456]{0:T(1024)(128)(4,1)} %bitcast.148), calls=%async_computation.9 | async-start | bytes 4194304
  153.7 18.8 %all-to-all-start.2 = ((bf16[3,512,256]{2,0,1:T(4,128)(2,1)}), bf16[3,512,256]{2,0,1:T(4,128)(2,1)}, u32[]{:S(2)}, u32[]{:S(2)}) async-start(bf16[3,512,256]{2,0,1:T(4,128)(2,1)} %pad_maximum_fusion.1), calls=%async_computation.2 | async-start | bytes 2097152 | tf_op jit(solution)/shard_map/all_to_all | solution.py:529
  167.2 7.0 %copy-start.29 = (f32[8,1024]{1,0:T(8,128)}, f32[8,1024]{1,0:T(8,128)S(1)}, u32[]{:S(2)}) copy-start(f32[8,1024]{1,0:T(8,128)S(1)} %scatter.9.refs_13_) | copy-start | bytes 98308
  167.2 7.2 %copy-start.8 = (f32[128,1024]{1,0:T(8,128)S(1)}, f32[128,1024]{1,0:T(8,128)}, u32[]{:S(2)}) copy-start(f32[128,1024]{1,0:T(8,128)} %copy-done.7) | copy-start | bytes 1572868
  167.2 7.2 %copy-start.14 = (bf16[1,128,1024]{2,1,0:T(8,128)(2,1)S(1)}, bf16[1,128,1024]{2,1,0:T(8,128)(2,1)}, u32[]{:S(2)}) copy-start(bf16[1,128,1024]{2,1,0:T(8,128)(2,1)} %param.33) | copy-start | bytes 786436
  195.8 5.1 %copy-start.15 = (bf16[2,512,1024]{2,1,0:T(8,128)(2,1)S(1)}, bf16[2,512,1024]{2,1,0:T(8,128)(2,1)}, u32[]{:S(2)}) copy-start(bf16[2,512,1024]{2,1,0:T(8,128)(2,1)} %all-gather.6.cloned.1.call-done) | copy-start | bytes 6291460
  202.5 106.5 %copy-start.1 = (bf16[1024,1024]{1,0:T(8,128)(2,1)S(1)}, bf16[1024,1024]{1,0:T(8,128)(2,1)}, u32[]{:S(2)}) copy-start(bf16[1024,1024]{1,0:T(8,128)(2,1)} %param.27) | copy-start | bytes 6291460
  296.6 10.8 %copy-start.25 = (f32[512,256]{1,0:T(8,128)S(1)}, f32[512,256]{1,0:T(8,128)}, u32[]{:S(2)}) copy-start(f32[512,256]{1,0:T(8,128)} %get-tuple-element.121) | copy-start | bytes 1572868
  296.6 11.6 %copy-start.26 = (f32[384,256]{1,0:T(8,128)S(1)}, f32[384,256]{1,0:T(8,128)}, u32[]{:S(2)}) copy-start(f32[384,256]{1,0:T(8,128)} %get-tuple-element.122) | copy-start | bytes 1179652
  (14 other events, 31.4 us)
Sparse Core Ops, SparseCore 0:
  12.0 31.2 all-gather.3
  77.9 23.1 reduce-scatter.1
  102.7 16.7 all-gather.7
  123.4 24.8 all-gather.5

commit v2 on v1

--- a/solution.py
+++ b/solution.py
@@ -202,15 +202,17 @@
 def ring_mm_kernel(seqs, tiers, plan, nfac, *refs):
     nparts = len(plan)
     facs = refs[:nfac]
-    g_ref = refs[nfac]
-    out_refs = refs[nfac + 1 : nfac + 1 + nparts]
-    gout_ref = refs[nfac + 1 + nparts]
-    scratch = refs[nfac + 2 + nparts :]
+    g_ref, seg_ref, wq_ref, wk_ref, wv_ref = refs[nfac : nfac + 5]
+    out_refs = refs[nfac + 5 : nfac + 5 + nparts]
+    gout_ref, terms_ref = refs[nfac + 5 + nparts : nfac + 7 + nparts]
+    scratch = refs[nfac + 7 + nparts :]
     recvs = scratch[:nparts]
     sbufs = scratch[nparts : 2 * nparts]
     owns = scratch[2 * nparts : 3 * nparts]
     (send_sem, recv_sem, free_sem, grecv, gsbuf, gsend_sem, grecv_sem, gfree_sem,
-     tsrc, trecv, tsend_sem, trecv_sem) = scratch[3 * nparts :]
+     tsrc, trecv, tsend_sem, trecv_sem, arecv, asend_sem, arecv_sem) = scratch[3 * nparts :]
+    own_rows = terms_ref.shape[0]
+    col_w = seg_ref.shape[2]
 
     me = lax.axis_index("seq")
     tier = lax.axis_index("tier")
@@ -238,6 +240,36 @@
         )
         cp.start()
         tcopies.append(cp)
+    acopies = []
+    for j in range(1, tiers):
+        peer = lax.rem(tier + j, tiers)
+        cp = pltpu.make_async_remote_copy(
+            src_ref=seg_ref.at[:, pl.ds(pl.multiple_of(peer * own_rows, own_rows), own_rows), :],
+            dst_ref=arecv.at[j - 1],
+            send_sem=asend_sem.at[j - 1],
+            recv_sem=arecv_sem.at[j - 1],
+            device_id=(me, peer),
+            device_id_type=MESH,
+        )
+        cp.start()
+        acopies.append(cp)
+
+    def input_terms():
+        w_refs = (wq_ref, wk_ref, wv_ref)
+        total = None
+        for j in range(tiers):
+            src = lax.rem(tier - j + tiers, tiers)
+            cols = pl.ds(pl.multiple_of(src * col_w, col_w), col_w)
+            for g in range(3):
+                if j == 0:
+                    x = seg_ref[g, pl.ds(pl.multiple_of(tier * own_rows, own_rows), own_rows), :]
+                else:
+                    x = arecv[j - 1, g]
+                term = lax.dot_general(
+                    x, w_refs[g][:, cols], (((1,), (1,)), ((), ())), preferred_element_type=f32
+                )
+                total = term if total is None else total + term
+        terms_ref[...] = total
 
     def block_of(d, k):
         if k == seqs - 1:
@@ -306,6 +338,10 @@
         )
         copies["g"].start()
         compute_own(k + 1)
+        if k == 0:
+            for cp in acopies:
+                cp.wait()
+            input_terms()
         for cp in copies.values():
             cp.wait_send()
     last = (seqs - 2) % 2
@@ -318,16 +354,19 @@
     gout_ref[...] = grecv[last] + tier_sum
 
 
-def ring_matmul_reduce(factors, plan, small, seqs, tiers):
+def ring_matmul_reduce(factors, plan, small, seg_grads, weights, seqs, tiers):
     nfac = len(factors)
     shapes = [(factors[a].shape[1] // seqs, factors[b].shape[1]) for a, b in plan]
     nparts = len(plan)
+    _, seg, col_w = seg_grads.shape
+    own_rows = seg // tiers
+    width = weights[0].shape[0]
     return pl.pallas_call(
         functools.partial(ring_mm_kernel, seqs, tiers, tuple(plan), nfac),
         out_shape=tuple(jax.ShapeDtypeStruct(sh, f32) for sh in shapes)
-        + (jax.ShapeDtypeStruct(small.shape, f32),),
-        in_specs=[pl.BlockSpec(memory_space=pltpu.VMEM)] * (nfac + 1),
-        out_specs=(pl.BlockSpec(memory_space=pltpu.VMEM),) * (nparts + 1),
+        + (jax.ShapeDtypeStruct(small.shape, f32), jax.ShapeDtypeStruct((own_rows, width), f32)),
+        in_specs=[pl.BlockSpec(memory_space=pltpu.VMEM)] * (nfac + 5),
+        out_specs=(pl.BlockSpec(memory_space=pltpu.VMEM),) * (nparts + 2),
         scratch_shapes=[pltpu.VMEM((2, 2, r, c // 2), bf16) for r, c in shapes]
         + [pltpu.VMEM((2, 2, r, c // 2), bf16) for r, c in shapes]
         + [pltpu.VMEM((2, r, c // 2), f32) for r, c in shapes]
@@ -344,11 +383,14 @@
             pltpu.VMEM((tiers - 1,) + small.shape, f32),
             pltpu.SemaphoreType.DMA((tiers - 1,)),
             pltpu.SemaphoreType.DMA((tiers - 1,)),
+            pltpu.VMEM((tiers - 1, 3, own_rows, col_w), bf16),
+            pltpu.SemaphoreType.DMA((tiers - 1,)),
+            pltpu.SemaphoreType.DMA((tiers - 1,)),
         ],
         compiler_params=pltpu.CompilerParams(
             collective_id=1, has_side_effects=True, vmem_limit_bytes=56 * 1024 * 1024
         ),
-    )(*factors, small)
+    )(*factors, small, seg_grads, *weights)
 
 
 def per_device(
@@ -526,11 +568,13 @@
         late_parts = (part_query, part_key, part_value)
 
     seg_grads = jnp.stack([grad_q, grad_k[2 * seg :], grad_v[2 * seg :]], axis=0)
-    own_grads = lax.all_to_all(seg_grads, "tier", 1, 2, tiled=True)
-    grad_hidden = grad_resid + mm_nt(own_grads[0], query_weight)
-    grad_hidden = grad_hidden + mm_nt(own_grads[1], key_weight)
-    grad_hidden = grad_hidden + mm_nt(own_grads[2], value_weight)
-    grad_input = grad_hidden * mask_own
+    fused = all((m // seqs) % 128 == 0 for m in (width, ff, 3 * width))
+    if not fused:
+        own_grads = lax.all_to_all(seg_grads, "tier", 1, 2, tiled=True)
+        grad_hidden = grad_resid + mm_nt(own_grads[0], query_weight)
+        grad_hidden = grad_hidden + mm_nt(own_grads[1], key_weight)
+        grad_hidden = grad_hidden + mm_nt(own_grads[2], value_weight)
+        grad_input = grad_hidden * mask_own
 
     slope_full = lax.dynamic_update_slice_in_dim(jnp.zeros((width,), f32), part_slope, tier_pos * hpt, 0)
     small = jnp.zeros((8, width), f32).at[0].set(part_gain).at[1].set(slope_full)
@@ -542,7 +586,10 @@
             jnp.pad(windows, ((0, comp_pad), (0, 0))), jnp.pad(grad_comp_t, ((0, comp_pad), (0, 0))),
         )
         plan = ((0, 1), (2, 3), (2, 4), (5, 6), (7, 8), (9, 10), (11, 12))
-        *outs, small_total = ring_matmul_reduce(factors, plan, small, seqs, tiers)
+        *outs, small_total, terms = ring_matmul_reduce(
+            factors, plan, small, seg_grads, (query_weight, key_weight, value_weight), seqs, tiers
+        )
+        grad_input = (grad_resid + terms) * mask_own
     else:
         late_parts = tuple(p.astype(bf16) for p in late_parts)
         *outs, small_total = ring_reduce_scatter(late_parts + early_parts, small, seqs, tiers)

time: 321 us -> 297 us (0.925)
  waiting for transfers between devices: 38.1 us -> 26 us
  local copies, waits for them, and re-layouts: 46.7 us -> 38.9 us
  Pallas kernels: 94.1 us -> 99.7 us
  matrix products: 84.7 us -> 80.4 us
  starting transfers between devices: 12 us -> 7.8 us
    pallas_call x1, Pallas kernels: 94.1 us -> 99.7 us  [ring_matmul_reduce(): pl.pallas_call(functools.partial(ring_mm_kernel, seqs, tiers, tuple(plan)...]
    all_to_all x1 -> x0, waiting for transfers between devices: 5.21 us -> none  [per_device(): own_grads = lax.all_to_all(seg_grads, 'tier', 1, 2, tiled=True)]
    dot_general x8 -> x5, matrix products: 20.1 us -> 15.1 us  [mm_nt(): lax.dot_general(left, right, (((1,), (1,)), ((), ())), preferred_element_...]
    all_to_all x1 -> x0, starting transfers between devices: 4.24 us -> none  [per_device(): own_grads = lax.all_to_all(seg_grads, 'tier', 1, 2, tiled=True)]
    all_to_all x1, waiting for transfers between devices: 4.8 us -> 0.77 us  [per_device(): lax.all_to_all(jnp.stack([grad_attended, grad_att], axis=0), 'tier', 2, 1...]
    unnamed x89 -> x95, local copies, waits for them, and re-layouts: 14.2 us -> 10.7 us
    dot_general x1, matrix products: 1.27 us -> 4.57 us  [per_device(): jnp.einsum('hrk,rhd->khd', probs_low, grad_att_h, preferred_element_type=...]
  transfers between devices with their start and end apart: 7 -> 6, of which waited for: 4 -> 3; matrix products, arithmetic and copies ran while one was open for 26% -> 25% of each run, Pallas kernels for 0% -> 0%
where the time goes in v2:
time: 297 us; the launch traced here: 293 us
  Pallas kernels  99.7 us (34%)
  matrix products  80.4 us (27%)
  local copies, waits for them, and re-layouts  38.9 us (13%)
  waiting for transfers between devices  26 us (9%)
  other arithmetic  23.8 us (8%)
  between operations  16.2 us (5%)
  starting transfers between devices  7.8 us (3%)
    pallas_call x1, Pallas kernels, ring_matmul_reduce(): pl.pallas_call(functools.partial(ring_mm_kernel, seqs, tiers, tuple(plan)...  99.7 us
    dot_general x8, matrix products, mm(): return jnp.dot(left, right, preferred_element_type=f32)  33.4 us
    all_gather x1, waiting for transfers between devices, per_device(): raw_seq = lax.all_gather(raw_local, 'tier', axis=1, tiled=True)  24.5 us
    dot_general x5, matrix products, mm_nt(): lax.dot_general(left, right, (((1,), (1,)), ((), ())), preferred_element_...  15.1 us
    unnamed x95, local copies, waits for them, and re-layouts  10.7 us
  transfers between devices with their start and end apart: 6, of which 3 were waited for; matrix products, arithmetic and copies ran while one was open for 25% of the time, Pallas kernels for 0%

profile of v2, /device:TPU:0, one launch (start us, length us, event | category | flops | bytes accessed | tf_op | source)
XLA Modules:
  0.0 292.8 jit_solution(7393532898245033358)
XLA Ops:
  9.8 2.0 pad_maximum_fusion.1
  14.0 1.7 fusion.14
  15.7 3.1 %fusion.42 = (f32[1536,512]{0,1:T(8,128)}, f32[512,1536]{1,0:T(8,128)}) fusion(s32[512]{0:T(512)S(1)} %iota_add_fusion), kind=kLoop, calls=%fused_computation.69 | loop fusion | flops 1572864 | bytes 6293504
  18.8 24.5 %all-gather.4.cloned.1.call-done = bf16[3,512,1024]{2,1,0:T(8,128)(2,1)} async-done(((bf16[3,128,1024]{2,1,0:T(8,128)(2,1)}), bf16[3,512,1024]{2,1,0:T(8,128)(2,1)}) %all-gather.4.cloned.1.call-update) | async-done | bytes 3145744 | tf_op jit(solution)/shard_map/all_gather | solution.py:437
  43.2 2.8 slice_bitcast_fusion.2
  46.1 1.8 convolution_convert_fusion
  52.4 2.5 reshape.315
  54.9 4.5 %convolution_convert_fusion.2 = bf16[171,1024]{1,0:T(8,128)(2,1)S(1)} fusion(bf16[171,3072]{1,0:T(8,128)(2,1)} %reshape.315, bf16[3072,1024]{1,0:T(8,128)(2,1)} %param.32), kind=kOutput, calls=%fused_computation.56 | convolution fusion | flops 1076014080 | bytes 7692288 | tf_op jit(solution)/shard_map/dot_general | solution.py:34
  62.2 1.8 fusion.126
  64.0 2.3 fusion.74
  66.3 3.0 %fusion.44 = bf16[512,2,128]{0,2,1:T(8,128)(2,1)} fusion(f32[2,128,512]{2,1,0:T(8,128)} %fusion.74, bf16[512,2,128]{0,2,1:T(8,128)(2,1)S(1)} %bitcast.174, f32[2,512]{1,0:T(2,128)S(1)} %fusion.126, f32[512]{0:T(512)S(1)} %fusion.89, bf16[512,2,128]{0,2,1:T(8,128)(2,1)S(1)} %bitcast.165, bf16[512,2,128]{0,2,1:T(8,128)(2,1)} %bitcast.173), kind=kOutput, calls=%fused_computation.72 | convolution fusion | flops 270927360 | bytes 1579008 | tf_op jit(solution)/shard_map/hrk,khd->rhd/dot_general | solution.py:478
  70.8 2.3 multiply_reduce_fusion.3
  75.2 2.6 fusion.59
  77.8 4.1 %fusion.121 = (f32[2,512]{1,0:T(2,128)S(1)}, f32[2,512,1536]{2,1,0:T(8,128)S(1)}) fusion(f32[512,1536]{1,0:T(8,128)} %get-tuple-element.78, f32[2]{0:T(128)S(1)} %dynamic_slice.27, bf16[512,2,128]{0,2,1:T(8,128)(2,1)S(1)} %bitcast.168, bf16[1536,2,128]{0,2,1:T(8,128)(2,1)S(1)} %bitcast.142, pred[512,1536]{1,0:T(8,128)(4,1)} %fusion.14), kind=kOutput, calls=%fused_computation.166 | convolution fusion | flops 410516480 | bytes 11276296 | tf_op jit(solution)/shard_map/rhd,khd->hrk/dot_general | solution.py:464
  86.9 3.4 %all-to-all-start = ((bf16[4,128,256]{2,1,0:T(8,128)(2,1)}), bf16[4,128,256]{2,1,0:T(8,128)(2,1)S(1)}, u32[]{:S(2)}, u32[]{:S(2)}) async-start(bf16[4,128,256]{2,1,0:T(8,128)(2,1)} %copy.104), calls=%async_computation | async-start | bytes 524288 | tf_op jit(solution)/shard_map/all_to_all | solution.py:472
  90.5 2.2 slice_bitcast_fusion.4
  93.9 2.0 fusion.66
  97.5 1.7 fusion.122
  99.6 6.3 %multiply_convert_fusion.2 = (bf16[128,4096]{1,0:T(8,128)(2,1)}, f32[128,4096]{1,0:T(8,128)S(1)}) fusion(bf16[128,1024]{1,0:T(8,128)(2,1)S(1)} %multiply_convert_fusion.4, bf16[1024,4096]{1,0:T(8,128)(2,1)} %param.28), kind=kOutput, calls=%fused_computation.50 | convolution fusion | flops 1078460416 | bytes 11796480 | tf_op jit(solution)/shard_map/dot_general | solution.py:34
  106.0 3.6 %fusion.22 = bf16[128,4096]{1,0:T(8,128)(2,1)S(1)} fusion(f32[128,4096]{1,0:T(8,128)S(1)} %get-tuple-element.84, bf16[4096,1024]{1,0:T(8,128)(2,1)S(1)} %bitcast.137, f32[128]{0:T(128)S(1)} %compare_convert_fusion, bf16[1,128,1024]{2,1,0:T(8,128)(2,1)S(1)} %copy-done.12), kind=kOutput, calls=%fused_computation.37 | convolution fusion | flops 1084620800 | bytes 11796992 | tf_op jit(solution)/shard_map/dot_general | solution.py:42
  109.6 3.0 %multiply_reduce_fusion.4 = (f32[1024]{0:T(1024)S(1)}, f32[128]{0:T(128)S(1)}, f32[128,1024]{1,0:T(8,128)S(1)}) fusion(f32[128,1024]{1,0:T(8,128)S(1)} %get-tuple-element.82, f32[128]{0:T(128)S(1)} %fusion.91, f32[128]{0:T(128)S(1)} %broadcast_multiply_fusion, f32[1024]{0:T(1024)S(1)} %copy-done.36, bf16[128,4096]{1,0:T(8,128)(2,1)S(1)} %fusion.22, ...), kind=kOutput, calls=%fused_computation.102 | convolution fusion | flops 1074658176 | bytes 10495488 | tf_op jit(solution)/shard_map/dot_general | solution.py:42
  115.9 3.6 %all-to-all-start.1 = ((bf16[2,128,1024]{1,0,2:T(2,128)(2,1)}), bf16[2,128,1024]{1,0,2:T(2,128)(2,1)S(1)}, u32[]{:S(2)}, u32[]{:S(2)}) async-start(bf16[2,128,1024]{1,0,2:T(2,128)(2,1)} %copy.106), calls=%async_computation.1 | async-start | bytes 1048576 | tf_op jit(solution)/shard_map/all_to_all | solution.py:525
  120.4 1.8 pad_maximum_fusion.4
  122.2 5.3 %fusion.46 = bf16[1,128,1024]{2,1,0:T(8,128)(2,1)} fusion(f32[128,1024]{1,0:T(8,128)S(1)} %get-tuple-element.82, bf16[128,4096]{1,0:T(8,128)(2,1)S(1)} %copy-done.11, bf16[4096,1024]{1,0:T(8,128)(2,1)} %param.29, f32[128]{0:T(128)S(1)} %compare_convert_fusion), kind=kOutput, calls=%fused_computation.74 | convolution fusion | flops 1074135040 | bytes 10224128 | tf_op jit(solution)/shard_map/dot_general | solution.py:34
  129.7 4.6 %convolution_convert_fusion.1 = bf16[2,128,1536]{2,1,0:T(8,128)(2,1)S(1)} fusion(bf16[512,2,128]{0,2,1:T(8,128)(2,1)S(1)} %copy.112, f32[2,512,1536]{2,1,0:T(8,128)} %copy-done.2, f32[2,512]{1,0:T(2,128)S(1)} %log_add_fusion), kind=kOutput, calls=%fused_computation.30 | convolution fusion | flops 406192128 | bytes 7344128 | tf_op jit(solution)/shard_map/hrk,rhd->khd/dot_general | solution.py:562
  134.5 4.6 %multiply_reduce_fusion.1 = (f32[2,512]{1,0:T(2,128)S(1)}, f32[2,512,1536]{2,1,0:T(8,128)S(1)}) fusion(f32[2,512,1536]{2,1,0:T(8,128)} %copy-done.2, f32[2,512]{1,0:T(2,128)S(1)} %log_add_fusion, bf16[512,2,128]{0,2,1:T(8,128)(2,1)S(1)} %copy.112, bf16[1536,2,128]{0,2,1:T(8,128)(2,1)S(1)} %bitcast.145), kind=kOutput, calls=%fused_computation.13 | convolution fusion | flops 407370752 | bytes 13639680 | tf_op jit(solution)/shard_map/rhd,khd->hrk/dot_general | solution.py:553
  139.1 4.8 %multiply_reduce_fusion = (f32[2]{0:T(128)S(1)}, bf16[2,512,1536]{2,1,0:T(8,128)(2,1)S(1)}) fusion(f32[1536,512]{0,1:T(8,128)S(1)} %copy-done.4, f32[2,512,1536]{2,1,0:T(8,128)S(1)} %get-tuple-element.87, f32[2,512]{1,0:T(2,128)S(1)} %get-tuple-element.86, f32[2,512,1536]{2,1,0:T(8,128)} %copy-done.2, f32[2,512]{1,0:T(2,128)S(1)} %log_add_fusion), kind=kLoop, calls=%fused_computation.11 | loop fusion | flops 11010046 | bytes 18882568 | tf_op jit(solution)/shard_map/hrk,rk->h/dot_general | solution.py:555
  145.6 3.0 %fusion.40 = bf16[2,128,512]{2,1,0:T(8,128)(2,1)S(1)} fusion(bf16[1536,2,128]{0,2,1:T(8,128)(2,1)S(1)} %bitcast.143, bf16[2,512,1536]{2,1,0:T(8,128)(2,1)} %copy-done.3), kind=kOutput, calls=%fused_computation.65 | convolution fusion | flops 402915328 | bytes 4194304 | tf_op jit(solution)/shard_map/hrk,khd->rhd/dot_general | solution.py:557
  157.1 11.8 %fusion.9 = (bf16[512,4096]{1,0:T(8,128)(2,1)}, f32[512,4096]{1,0:T(8,128)S(1)}) fusion(bf16[1024,4096]{1,0:T(8,128)(2,1)} %param.28, bf16[2,512,1024]{2,1,0:T(8,128)(2,1)} %all-gather.6.cloned.1.call-done), kind=kOutput, calls=%fused_computation.10 | convolution fusion | flops 4313841664 | bytes 22020096 | tf_op jit(solution)/shard_map/dot_general | solution.py:34
  168.9 5.1 %fusion.29.refs_8_ = bf16[512,1024]{1,0:T(8,128)(2,1)} fusion(f32[512,4096]{1,0:T(8,128)S(1)} %get-tuple-element.89, s32[]{:T(128)S(6)} %select_n.38, bf16[512,1024]{1,0:T(8,128)(2,1)S(1)} %multiply_convert_fusion.1, bf16[4096,1024]{1,0:T(8,128)(2,1)} %param.29), kind=kOutput, calls=%fused_computation.44 | convolution fusion | flops 1084227584 | bytes 6292480 | tf_op jit(solution)/shard_map/dot_general | solution.py:42
  175.6 99.7 %shard_map.246 = (f32[128,256]{1,0:T(8,128)}, f32[128,256]{1,0:T(8,128)}, f32[128,256]{1,0:T(8,128)}, f32[128,256]{1,0:T(8,128)}, f32[128,1024]{1,0:T(8,128)}, /...) custom-call(bf16[512,1024]{1,0:T(8,128)(2,1)} %get-tuple-element.66.refs_0_, ...), custom_call_target="tpu_custom_call" | custom-call | tf_op jit(solution)/shard_map/pallas_call | solution.py:364
  278.0 2.2 multiply_bitcast_fusion
  (177 shorter events, 49.0 us)
Async XLA Ops:
  7.2 90.3 %copy-start = (bf16[1024,1024]{1,0:T(8,128)(2,1)S(1)}, bf16[1024,1024]{1,0:T(8,128)(2,1)}, u32[]{:S(2)}) copy-start(bf16[1024,1024]{1,0:T(8,128)(2,1)} %param.27) | copy-start | bytes 6291460
  7.2 5.4 %copy-start.37 = (f32[8]{0:T(128)S(1)}, f32[8]{0:T(128)}, u32[]{:S(2)}) copy-start(f32[8]{0:T(128)} %param.31) | copy-start | bytes 100
  7.2 36.0 %all-gather.4.cloned.1.call-start = ((), (), s32[]{:S(2)}) async-start(), calls=%async_computation.3 | async-start | bytes 3932160 | tf_op jit(solution)/shard_map/all_gather | solution.py:437
  11.9 141.5 %reduce-scatter.2.cloned.1.call-start = ((), (), s32[]{:S(2)}) async-start(), calls=%async_computation.6 | async-start | bytes 901120 | tf_op jit(solution)/shard_map/reduce_scatter | solution.py:500
  13.9 32.1 %copy-start.21 = (bf16[1024,256]{1,0:T(8,128)(2,1)}, bf16[1024,256]{1,0:T(8,128)(2,1)S(1)}, u32[]{:S(2)}) copy-start(bf16[1024,256]{1,0:T(8,128)(2,1)S(1)} %get-tuple-element.94) | copy-start | bytes 1572868
  14.0 32.1 %copy-start.23 = (bf16[1024,256]{1,0:T(8,128)(2,1)}, bf16[1024,256]{1,0:T(8,128)(2,1)S(1)}, u32[]{:S(2)}) copy-start(bf16[1024,256]{1,0:T(8,128)(2,1)S(1)} %get-tuple-element.95) | copy-start | bytes 1572868
  51.3 26.5 %copy-start.19 = (bf16[512,256]{0,1:T(8,128)(2,1)}, bf16[512,256]{0,1:T(8,128)(2,1)S(1)}, u32[]{:S(2)}) copy-start(bf16[512,256]{0,1:T(8,128)(2,1)S(1)} %convolution_convert_fusion.5) | copy-start | bytes 786436
  60.3 6.1 %copy-start.34 = (bf16[171,2,128]{2,1,0:T(2,128)(2,1)}, bf16[171,2,128]{2,1,0:T(2,128)(2,1)S(1)}, u32[]{:S(2)}) copy-start(bf16[171,2,128]{2,1,0:T(2,128)(2,1)S(1)} %reshape.316) | copy-start | bytes 262660
  86.9 9.8 %all-to-all-start = ((bf16[4,128,256]{2,1,0:T(8,128)(2,1)}), bf16[4,128,256]{2,1,0:T(8,128)(2,1)S(1)}, u32[]{:S(2)}, u32[]{:S(2)}) async-start(bf16[4,128,256]{2,1,0:T(8,128)(2,1)} %copy.104), calls=%async_computation | async-start | bytes 524288 | tf_op jit(solution)/shard_map/all_to_all | solution.py:472
  90.3 64.7 %all-gather.8.cloned.1.call-start = ((), (), s32[]{:S(2)}) async-start(), calls=%async_computation.5 | async-start | bytes 1310720 | tf_op jit(solution)/shard_map/all_gather | solution.py:439
  97.5 8.5 %slice-start = ((s8[8388608]{0:T(1024)(128)(4,1)}), s8[4194304]{0:T(1024)(128)(4,1)S(1)}, s32[]{:S(2)}) async-start(s8[8388608]{0:T(1024)(128)(4,1)} %bitcast.136), calls=%async_computation.7 | async-start | bytes 8388608
  99.6 6.4 %copy-start.18 = (bf16[128,1024]{1,0:T(8,128)(2,1)}, bf16[128,1024]{1,0:T(8,128)(2,1)S(1)}, u32[]{:S(2)}) copy-start(bf16[128,1024]{1,0:T(8,128)(2,1)S(1)} %multiply_convert_fusion.4) | copy-start | bytes 786436
  99.6 6.4 %slice-start.1 = ((s8[8388608]{0:T(1024)(128)(4,1)}), s8[4194304]{0:T(1024)(128)(4,1)S(1)}, s32[]{:S(2)}) async-start(s8[8388608]{0:T(1024)(128)(4,1)} %bitcast.136), calls=%async_computation.8 | async-start | bytes 8388608
  99.6 6.4 %copy-start.12 = (bf16[1,128,1024]{2,1,0:T(8,128)(2,1)S(1)}, bf16[1,128,1024]{2,1,0:T(8,128)(2,1)}, u32[]{:S(2)}) copy-start(bf16[1,128,1024]{2,1,0:T(8,128)(2,1)} %param.33) | copy-start | bytes 786436
  99.6 10.0 %slice-start.2 = ((s8[8388608]{0:T(1024)(128)(4,1)}), s8[4194304]{0:T(1024)(128)(4,1)S(1)}, s32[]{:S(2)}) async-start(s8[8388608]{0:T(1024)(128)(4,1)} %bitcast.140), calls=%async_computation.9 | async-start | bytes 8388608
  114.7 5.3 %copy-start.15 = (bf16[4,128,256]{2,1,0:T(8,128)(2,1)S(1)}, bf16[4,128,256]{2,1,0:T(8,128)(2,1)}, u32[]{:S(2)}) copy-start(bf16[4,128,256]{2,1,0:T(8,128)(2,1)} %copy-done.14) | copy-start | bytes 786436
  115.9 6.3 %copy-start.11 = (bf16[128,4096]{1,0:T(8,128)(2,1)S(1)}, bf16[128,4096]{1,0:T(8,128)(2,1)}, u32[]{:S(2)}) copy-start(bf16[128,4096]{1,0:T(8,128)(2,1)} %get-tuple-element.83) | copy-start | bytes 3145732
  115.9 12.4 %all-to-all-start.1 = ((bf16[2,128,1024]{1,0,2:T(2,128)(2,1)}), bf16[2,128,1024]{1,0,2:T(2,128)(2,1)S(1)}, u32[]{:S(2)}, u32[]{:S(2)}) async-start(bf16[2,128,1024]{1,0,2:T(2,128)(2,1)} %copy.106), calls=%async_computation.1 | async-start | bytes 1048576 | tf_op jit(solution)/shard_map/all_to_all | solution.py:525
  119.5 37.7 %all-gather.6.cloned.1.call-start = ((), (), s32[]{:S(2)}) async-start(), calls=%async_computation.4 | async-start | bytes 2621440 | tf_op jit(solution)/shard_map/all_gather | solution.py:529
  129.7 4.8 %copy-start.7 = (bf16[1536,256]{0,1:T(8,128)(2,1)S(1)}, bf16[1536,256]{0,1:T(8,128)(2,1)}, u32[]{:S(2)}) copy-start(bf16[1536,256]{0,1:T(8,128)(2,1)} %get-tuple-element.72) | copy-start | bytes 2359300
  139.1 4.8 %copy-start.20 = (bf16[512,256]{0,1:T(8,128)(2,1)S(1)}, bf16[512,256]{0,1:T(8,128)(2,1)}, u32[]{:S(2)}) copy-start(bf16[512,256]{0,1:T(8,128)(2,1)} %copy-done.19) | copy-start | bytes 786436
  152.4 4.8 %copy-start.30 = (f32[8,1024]{1,0:T(8,128)}, f32[8,1024]{1,0:T(8,128)S(1)}, u32[]{:S(2)}) copy-start(f32[8,1024]{1,0:T(8,128)S(1)} %scatter.9.refs_13_) | copy-start | bytes 98308
  168.9 5.1 %copy-start.16 = (bf16[2,512,1024]{2,1,0:T(8,128)(2,1)S(1)}, bf16[2,512,1024]{2,1,0:T(8,128)(2,1)}, u32[]{:S(2)}) copy-start(bf16[2,512,1024]{2,1,0:T(8,128)(2,1)} %all-gather.6.cloned.1.call-done) | copy-start | bytes 6291460
  175.6 102.4 %copy-start.9 = (f32[128,1024]{1,0:T(8,128)S(1)}, f32[128,1024]{1,0:T(8,128)}, u32[]{:S(2)}) copy-start(f32[128,1024]{1,0:T(8,128)} %copy-done.8) | copy-start | bytes 1572868
  175.6 102.4 %copy-start.13 = (bf16[1,128,1024]{2,1,0:T(8,128)(2,1)S(1)}, bf16[1,128,1024]{2,1,0:T(8,128)(2,1)}, u32[]{:S(2)}) copy-start(bf16[1,128,1024]{2,1,0:T(8,128)(2,1)} %param.33) | copy-start | bytes 786436
  275.3 6.4 %copy-start.33 = (f32[128,256]{1,0:T(8,128)S(1)}, f32[128,256]{1,0:T(8,128)}, u32[]{:S(2)}) copy-start(f32[128,256]{1,0:T(8,128)} %get-tuple-element.116) | copy-start | bytes 393220
  275.3 7.1 %copy-start.32 = (f32[128,256]{1,0:T(8,128)S(1)}, f32[128,256]{1,0:T(8,128)}, u32[]{:S(2)}) copy-start(f32[128,256]{1,0:T(8,128)} %get-tuple-element.117) | copy-start | bytes 393220
  275.3 7.7 %copy-start.31 = (f32[128,256]{1,0:T(8,128)S(1)}, f32[128,256]{1,0:T(8,128)}, u32[]{:S(2)}) copy-start(f32[128,256]{1,0:T(8,128)} %get-tuple-element.118) | copy-start | bytes 393220
  275.3 8.4 %copy-start.26 = (f32[128,1024]{1,0:T(8,128)S(1)}, f32[128,1024]{1,0:T(8,128)}, u32[]{:S(2)}) copy-start(f32[128,1024]{1,0:T(8,128)} %get-tuple-element.119) | copy-start | bytes 1572868
  275.4 9.2 %copy-start.25 = (f32[512,256]{1,0:T(8,128)S(1)}, f32[512,256]{1,0:T(8,128)}, u32[]{:S(2)}) copy-start(f32[512,256]{1,0:T(8,128)} %get-tuple-element.120) | copy-start | bytes 1572868
  278.0 7.3 %copy-start.27 = (f32[384,256]{1,0:T(8,128)S(1)}, f32[384,256]{1,0:T(8,128)}, u32[]{:S(2)}) copy-start(f32[384,256]{1,0:T(8,128)} %get-tuple-element.121) | copy-start | bytes 1179652
  278.0 8.1 %copy-start.1 = (bf16[1024,1024]{1,0:T(8,128)(2,1)S(1)}, bf16[1024,1024]{1,0:T(8,128)(2,1)}, u32[]{:S(2)}) copy-start(bf16[1024,1024]{1,0:T(8,128)(2,1)} %param.27) | copy-start | bytes 6291460
  (16 other events, 39.7 us)
Sparse Core Ops, SparseCore 0:
  12.0 31.2 all-gather.3
  77.9 23.1 reduce-scatter.1
  102.7 16.7 all-gather.7
  122.3 23.7 all-gather.5

commit v3 on v2

--- a/solution.py
+++ b/solution.py
@@ -281,10 +281,17 @@
     def compute_own(k):
         for d in range(2):
             blk = block_of(d, k)
-            for i, (ai, bi) in enumerate(plan):
+            for i, entry in enumerate(plan):
                 rows, cols = out_refs[i].shape
                 half = cols // 2
-                a_blk = facs[ai][:, pl.ds(pl.multiple_of(blk * rows, rows), rows)]
+                blk_cols = pl.ds(pl.multiple_of(blk * rows, rows), rows)
+                if len(entry) == 3:
+                    ai, wi, bi = entry
+                    pre = jnp.dot(facs[ai][...], facs[wi][:, blk_cols], preferred_element_type=f32)
+                    a_blk = gelu_tanh(pre).astype(bf16)
+                else:
+                    ai, bi = entry
+                    a_blk = facs[ai][:, blk_cols]
                 b_half = facs[bi][:, pl.ds(d * half, half)]
                 owns[i][d] = lax.dot_general(
                     a_blk, b_half, (((0,), (0,)), ((), ())), preferred_element_type=f32
@@ -356,7 +363,7 @@
 
 def ring_matmul_reduce(factors, plan, small, seg_grads, weights, seqs, tiers):
     nfac = len(factors)
-    shapes = [(factors[a].shape[1] // seqs, factors[b].shape[1]) for a, b in plan]
+    shapes = [(factors[e[-2]].shape[1] // seqs, factors[e[-1]].shape[1]) for e in plan]
     nparts = len(plan)
     _, seg, col_w = seg_grads.shape
     own_rows = seg // tiers
@@ -530,17 +537,16 @@
     normed_seq = fwd_seq[0]
     attended_seq = fwd_seq[1]
     grad_seq = (cot_seq.astype(f32) * mask_all).astype(bf16)
-    pre_seq = mm(normed_seq, ffn_in_weight)
-    act_seq = gelu_tanh(pre_seq).astype(bf16)
+    fused = all((m // seqs) % 128 == 0 for m in (width, ff, 3 * width))
     fcol0 = tier_pos * ffb
-    pre_seq_t = lax.dynamic_slice_in_dim(pre_seq, fcol0, ffb, axis=1)
+    pre_seq_t = mm(normed_seq, lax.dynamic_slice_in_dim(ffn_in_weight, fcol0, ffb, axis=1))
     wfo_t = lax.dynamic_slice_in_dim(ffn_out_weight, fcol0, ffb, axis=0)
     grad_act_seq_t = mm_nt(grad_seq, wfo_t)
     _, gelu_pull_seq = jax.vjp(gelu_tanh, pre_seq_t)
     grad_pre_seq_t = gelu_pull_seq(grad_act_seq_t)[0].astype(bf16)
     grad_seq_t = lax.dynamic_slice_in_dim(grad_seq, col0, cb, axis=1)
-    fused = all((m // seqs) % 128 == 0 for m in (width, ff, 3 * width))
     if not fused:
+        act_seq = gelu_tanh(mm(normed_seq, ffn_in_weight)).astype(bf16)
         part_comp = mm_tn(windows, grad_comp_t)
         part_ffn_in = mm_tn(normed_seq, grad_pre_seq_t)
         part_ffn_out = mm_tn(act_seq, grad_seq_t)
@@ -568,7 +574,6 @@
         late_parts = (part_query, part_key, part_value)
 
     seg_grads = jnp.stack([grad_q, grad_k[2 * seg :], grad_v[2 * seg :]], axis=0)
-    fused = all((m // seqs) % 128 == 0 for m in (width, ff, 3 * width))
     if not fused:
         own_grads = lax.all_to_all(seg_grads, "tier", 1, 2, tiled=True)
         grad_hidden = grad_resid + mm_nt(own_grads[0], query_weight)
@@ -582,10 +587,10 @@
         comp_pad = (-ncomp) % 16
         factors = (
             hidden_seq, grad_q, context, grad_k, grad_v, attended_seq, grad_att_t,
-            normed_seq, grad_pre_seq_t, act_seq, grad_seq_t,
+            normed_seq, grad_pre_seq_t, ffn_in_weight, grad_seq_t,
             jnp.pad(windows, ((0, comp_pad), (0, 0))), jnp.pad(grad_comp_t, ((0, comp_pad), (0, 0))),
         )
-        plan = ((0, 1), (2, 3), (2, 4), (5, 6), (7, 8), (9, 10), (11, 12))
+        plan = ((0, 1), (2, 3), (2, 4), (5, 6), (7, 8), (7, 9, 10), (11, 12))
         *outs, small_total, terms = ring_matmul_reduce(
             factors, plan, small, seg_grads, (query_weight, key_weight, value_weight), seqs, tiers
         )

time: 297 us -> 290 us (0.976)
  matrix products: 80.4 us -> 71.9 us
    dot_general x8, matrix products: 33.4 us -> 24.8 us  [mm(): return jnp.dot(left, right, preferred_element_type=f32)]
where the time goes in v3:
time: 290 us; the launch traced here: 286 us
  Pallas kernels  101 us (35%)
  matrix products  71.9 us (25%)
  local copies, waits for them, and re-layouts  38.9 us (13%)
  waiting for transfers between devices  26.1 us (9%)
  other arithmetic  23.8 us (8%)
  between operations  16.2 us (6%)
  starting transfers between devices  7.79 us (3%)
    pallas_call x1, Pallas kernels, ring_matmul_reduce(): pl.pallas_call(functools.partial(ring_mm_kernel, seqs, tiers, tuple(plan)...  101 us
    dot_general x8, matrix products, mm(): return jnp.dot(left, right, preferred_element_type=f32)  24.8 us
    all_gather x1, waiting for transfers between devices, per_device(): raw_seq = lax.all_gather(raw_local, 'tier', axis=1, tiled=True)  24.5 us
    dot_general x5, matrix products, mm_nt(): lax.dot_general(left, right, (((1,), (1,)), ((), ())), preferred_element_...  15.1 us
    unnamed x95, local copies, waits for them, and re-layouts  10.7 us
  transfers between devices with their start and end apart: 6, of which 3 were waited for; matrix products, arithmetic and copies ran while one was open for 25% of the time, Pallas kernels for 0%

profile of v3, /device:TPU:0, one launch (start us, length us, event | category | flops | bytes accessed | tf_op | source)
XLA Modules:
  0.0 285.6 jit_solution(5894219146124491210)
XLA Ops:
  9.8 2.0 pad_maximum_fusion.1
  14.0 1.7 fusion.6
  15.7 3.1 %fusion.36 = (f32[1536,512]{0,1:T(8,128)}, f32[512,1536]{1,0:T(8,128)}) fusion(s32[512]{0:T(512)S(1)} %iota_add_fusion), kind=kLoop, calls=%fused_computation.62 | loop fusion | flops 1572864 | bytes 6293504
  18.8 24.5 %all-gather.4.cloned.1.call-done = bf16[3,512,1024]{2,1,0:T(8,128)(2,1)} async-done(((bf16[3,128,1024]{2,1,0:T(8,128)(2,1)}), bf16[3,512,1024]{2,1,0:T(8,128)(2,1)}) %all-gather.4.cloned.1.call-update) | async-done | bytes 3145744 | tf_op jit(solution)/shard_map/all_gather | solution.py:444
  43.2 2.8 slice_bitcast_fusion.2
  46.1 1.8 convolution_convert_fusion
  52.4 2.5 reshape.315
  54.9 4.5 %convolution_convert_fusion.2 = bf16[171,1024]{1,0:T(8,128)(2,1)S(1)} fusion(bf16[171,3072]{1,0:T(8,128)(2,1)} %reshape.315, bf16[3072,1024]{1,0:T(8,128)(2,1)} %param.32), kind=kOutput, calls=%fused_computation.49 | convolution fusion | flops 1076014080 | bytes 7692288 | tf_op jit(solution)/shard_map/dot_general | solution.py:34
  62.2 1.8 fusion.120
  64.0 2.3 fusion.68
  66.3 3.0 %fusion.38 = bf16[512,2,128]{0,2,1:T(8,128)(2,1)} fusion(f32[2,128,512]{2,1,0:T(8,128)} %fusion.68, bf16[512,2,128]{0,2,1:T(8,128)(2,1)S(1)} %bitcast.171, f32[2,512]{1,0:T(2,128)S(1)} %fusion.120, f32[512]{0:T(512)S(1)} %fusion.84, bf16[512,2,128]{0,2,1:T(8,128)(2,1)S(1)} %bitcast.162, bf16[512,2,128]{0,2,1:T(8,128)(2,1)} %bitcast.170), kind=kOutput, calls=%fused_computation.65 | convolution fusion | flops 270927360 | bytes 1579008 | tf_op jit(solution)/shard_map/hrk,khd->rhd/dot_general | solution.py:485
  70.8 2.3 multiply_reduce_fusion.3
  75.2 2.6 fusion.53
  77.8 4.1 %fusion.115 = (f32[2,512]{1,0:T(2,128)S(1)}, f32[2,512,1536]{2,1,0:T(8,128)S(1)}) fusion(f32[512,1536]{1,0:T(8,128)} %get-tuple-element.78, f32[2]{0:T(128)S(1)} %dynamic_slice.27, bf16[512,2,128]{0,2,1:T(8,128)(2,1)S(1)} %bitcast.165, bf16[1536,2,128]{0,2,1:T(8,128)(2,1)S(1)} %bitcast.139, pred[512,1536]{1,0:T(8,128)(4,1)} %fusion.6), kind=kOutput, calls=%fused_computation.159 | convolution fusion | flops 410516480 | bytes 11276296 | tf_op jit(solution)/shard_map/rhd,khd->hrk/dot_general | solution.py:471
  86.9 3.4 %all-to-all-start = ((bf16[4,128,256]{2,1,0:T(8,128)(2,1)}), bf16[4,128,256]{2,1,0:T(8,128)(2,1)S(1)}, u32[]{:S(2)}, u32[]{:S(2)}) async-start(bf16[4,128,256]{2,1,0:T(8,128)(2,1)} %copy.104), calls=%async_computation | async-start | bytes 524288 | tf_op jit(solution)/shard_map/all_to_all | solution.py:479
  90.6 2.2 slice_bitcast_fusion.4
  93.9 2.0 fusion.60
  97.6 1.7 fusion.116
  99.7 6.3 %multiply_convert_fusion.2 = (bf16[128,4096]{1,0:T(8,128)(2,1)}, f32[128,4096]{1,0:T(8,128)S(1)}) fusion(bf16[128,1024]{1,0:T(8,128)(2,1)S(1)} %multiply_convert_fusion.4, bf16[1024,4096]{1,0:T(8,128)(2,1)} %refs_9_.1), kind=kOutput, calls=%fused_computation.43 | convolution fusion | flops 1078460416 | bytes 11796480 | tf_op jit(solution)/shard_map/dot_general | solution.py:34
  106.1 3.6 %fusion.14 = bf16[128,4096]{1,0:T(8,128)(2,1)S(1)} fusion(f32[128,4096]{1,0:T(8,128)S(1)} %get-tuple-element.84, bf16[4096,1024]{1,0:T(8,128)(2,1)S(1)} %bitcast.136, f32[128]{0:T(128)S(1)} %compare_convert_fusion, bf16[1,128,1024]{2,1,0:T(8,128)(2,1)S(1)} %copy-done.12), kind=kOutput, calls=%fused_computation.28 | convolution fusion | flops 1084620800 | bytes 11796992 | tf_op jit(solution)/shard_map/dot_general | solution.py:42
  109.7 3.0 %multiply_reduce_fusion.4 = (f32[1024]{0:T(1024)S(1)}, f32[128]{0:T(128)S(1)}, f32[128,1024]{1,0:T(8,128)S(1)}) fusion(f32[128,1024]{1,0:T(8,128)S(1)} %get-tuple-element.82, f32[128]{0:T(128)S(1)} %fusion.86, f32[128]{0:T(128)S(1)} %broadcast_multiply_fusion, f32[1024]{0:T(1024)S(1)} %copy-done.36, bf16[128,4096]{1,0:T(8,128)(2,1)S(1)} %fusion.14, ...), kind=kOutput, calls=%fused_computation.95 | convolution fusion | flops 1074658176 | bytes 10495488 | tf_op jit(solution)/shard_map/dot_general | solution.py:42
  116.0 3.6 %all-to-all-start.1 = ((bf16[2,128,1024]{1,0,2:T(2,128)(2,1)}), bf16[2,128,1024]{1,0,2:T(2,128)(2,1)S(1)}, u32[]{:S(2)}, u32[]{:S(2)}) async-start(bf16[2,128,1024]{1,0,2:T(2,128)(2,1)} %copy.106), calls=%async_computation.1 | async-start | bytes 1048576 | tf_op jit(solution)/shard_map/all_to_all | solution.py:532
  120.5 1.8 pad_maximum_fusion.4
  122.3 5.3 %fusion.40 = bf16[1,128,1024]{2,1,0:T(8,128)(2,1)} fusion(f32[128,1024]{1,0:T(8,128)S(1)} %get-tuple-element.82, bf16[128,4096]{1,0:T(8,128)(2,1)S(1)} %copy-done.11, bf16[4096,1024]{1,0:T(8,128)(2,1)} %param.29, f32[128]{0:T(128)S(1)} %compare_convert_fusion), kind=kOutput, calls=%fused_computation.67 | convolution fusion | flops 1074135040 | bytes 10224128 | tf_op jit(solution)/shard_map/dot_general | solution.py:34
  129.8 4.6 %convolution_convert_fusion.1 = bf16[2,128,1536]{2,1,0:T(8,128)(2,1)S(1)} fusion(bf16[512,2,128]{0,2,1:T(8,128)(2,1)S(1)} %copy.112, f32[2,512,1536]{2,1,0:T(8,128)} %copy-done.2, f32[2,512]{1,0:T(2,128)S(1)} %log_add_fusion), kind=kOutput, calls=%fused_computation.21 | convolution fusion | flops 406192128 | bytes 7344128 | tf_op jit(solution)/shard_map/hrk,rhd->khd/dot_general | solution.py:568
  134.6 4.6 %multiply_reduce_fusion.1 = (f32[2,512]{1,0:T(2,128)S(1)}, f32[2,512,1536]{2,1,0:T(8,128)S(1)}) fusion(f32[2,512,1536]{2,1,0:T(8,128)} %copy-done.2, f32[2,512]{1,0:T(2,128)S(1)} %log_add_fusion, bf16[512,2,128]{0,2,1:T(8,128)(2,1)S(1)} %copy.112, bf16[1536,2,128]{0,2,1:T(8,128)(2,1)S(1)} %bitcast.142), kind=kOutput, calls=%fused_computation.4 | convolution fusion | flops 407370752 | bytes 13639680 | tf_op jit(solution)/shard_map/rhd,khd->hrk/dot_general | solution.py:559
  139.2 4.8 %multiply_reduce_fusion = (f32[2]{0:T(128)S(1)}, bf16[2,512,1536]{2,1,0:T(8,128)(2,1)S(1)}) fusion(f32[1536,512]{0,1:T(8,128)S(1)} %copy-done.4, f32[2,512,1536]{2,1,0:T(8,128)S(1)} %get-tuple-element.87, f32[2,512]{1,0:T(2,128)S(1)} %get-tuple-element.86, f32[2,512,1536]{2,1,0:T(8,128)} %copy-done.2, f32[2,512]{1,0:T(2,128)S(1)} %log_add_fusion), kind=kLoop, calls=%fused_computation.2 | loop fusion | flops 11010046 | bytes 18882568 | tf_op jit(solution)/shard_map/hrk,rk->h/dot_general | solution.py:561
  145.8 3.0 %fusion.34 = bf16[2,128,512]{2,1,0:T(8,128)(2,1)S(1)} fusion(bf16[1536,2,128]{0,2,1:T(8,128)(2,1)S(1)} %bitcast.140, bf16[2,512,1536]{2,1,0:T(8,128)(2,1)} %copy-done.3), kind=kOutput, calls=%fused_computation.58 | convolution fusion | flops 402915328 | bytes 4194304 | tf_op jit(solution)/shard_map/hrk,khd->rhd/dot_general | solution.py:563
  157.3 3.2 %fusion.22 = f32[512,1024]{1,0:T(8,128)S(1)} fusion(bf16[1024,4096]{1,0:T(8,128)(2,1)} %refs_9_.1, s32[]{:T(128)S(6)} %select_n.38, bf16[2,512,1024]{2,1,0:T(8,128)(2,1)} %all-gather.6.cloned.1.call-done), kind=kOutput, calls=%fused_computation.38 | convolution fusion | flops 1073741824 | bytes 5242884 | tf_op jit(solution)/shard_map/dot_general | solution.py:34
  160.5 5.1 %fusion.21.refs_8_ = bf16[512,1024]{1,0:T(8,128)(2,1)} fusion(f32[512,1024]{1,0:T(8,128)S(1)} %fusion.22, bf16[512,1024]{1,0:T(8,128)(2,1)S(1)} %multiply_convert_fusion.1, bf16[4096,1024]{1,0:T(8,128)(2,1)} %param.29, s32[]{:T(128)S(6)} %select_n.38), kind=kOutput, calls=%fused_computation.35 | convolution fusion | flops 1084227584 | bytes 6291460 | tf_op jit(solution)/shard_map/dot_general | solution.py:42
  167.2 100.8 %shard_map.246 = (f32[128,256]{1,0:T(8,128)}, f32[128,256]{1,0:T(8,128)}, f32[128,256]{1,0:T(8,128)}, f32[128,256]{1,0:T(8,128)}, f32[128,1024]{1,0:T(8,128)}, /...) custom-call(bf16[512,1024]{1,0:T(8,128)(2,1)} %get-tuple-element.66.refs_0_, ...), custom_call_target="tpu_custom_call" | custom-call | tf_op jit(solution)/shard_map/pallas_call | solution.py:371
  270.7 2.2 multiply_bitcast_fusion
  (177 shorter events, 49.1 us)
Async XLA Ops:
  7.2 90.4 %copy-start = (bf16[1024,1024]{1,0:T(8,128)(2,1)S(1)}, bf16[1024,1024]{1,0:T(8,128)(2,1)}, u32[]{:S(2)}) copy-start(bf16[1024,1024]{1,0:T(8,128)(2,1)} %param.27) | copy-start | bytes 6291460
  7.2 5.4 %copy-start.37 = (f32[8]{0:T(128)S(1)}, f32[8]{0:T(128)}, u32[]{:S(2)}) copy-start(f32[8]{0:T(128)} %param.31) | copy-start | bytes 100
  7.2 36.0 %all-gather.4.cloned.1.call-start = ((), (), s32[]{:S(2)}) async-start(), calls=%async_computation.3 | async-start | bytes 3932160 | tf_op jit(solution)/shard_map/all_gather | solution.py:444
  11.8 141.7 %reduce-scatter.2.cloned.1.call-start = ((), (), s32[]{:S(2)}) async-start(), calls=%async_computation.6 | async-start | bytes 901120 | tf_op jit(solution)/shard_map/reduce_scatter | solution.py:507
  13.9 32.1 %copy-start.21 = (bf16[1024,256]{1,0:T(8,128)(2,1)}, bf16[1024,256]{1,0:T(8,128)(2,1)S(1)}, u32[]{:S(2)}) copy-start(bf16[1024,256]{1,0:T(8,128)(2,1)S(1)} %get-tuple-element.92) | copy-start | bytes 1572868
  14.0 32.1 %copy-start.23 = (bf16[1024,256]{1,0:T(8,128)(2,1)}, bf16[1024,256]{1,0:T(8,128)(2,1)S(1)}, u32[]{:S(2)}) copy-start(bf16[1024,256]{1,0:T(8,128)(2,1)S(1)} %get-tuple-element.93) | copy-start | bytes 1572868
  51.3 26.5 %copy-start.19 = (bf16[512,256]{0,1:T(8,128)(2,1)}, bf16[512,256]{0,1:T(8,128)(2,1)S(1)}, u32[]{:S(2)}) copy-start(bf16[512,256]{0,1:T(8,128)(2,1)S(1)} %convolution_convert_fusion.5) | copy-start | bytes 786436
  60.3 6.1 %copy-start.34 = (bf16[171,2,128]{2,1,0:T(2,128)(2,1)}, bf16[171,2,128]{2,1,0:T(2,128)(2,1)S(1)}, u32[]{:S(2)}) copy-start(bf16[171,2,128]{2,1,0:T(2,128)(2,1)S(1)} %reshape.316) | copy-start | bytes 262660
  86.9 9.8 %all-to-all-start = ((bf16[4,128,256]{2,1,0:T(8,128)(2,1)}), bf16[4,128,256]{2,1,0:T(8,128)(2,1)S(1)}, u32[]{:S(2)}, u32[]{:S(2)}) async-start(bf16[4,128,256]{2,1,0:T(8,128)(2,1)} %copy.104), calls=%async_computation | async-start | bytes 524288 | tf_op jit(solution)/shard_map/all_to_all | solution.py:479
  90.3 64.8 %all-gather.8.cloned.1.call-start = ((), (), s32[]{:S(2)}) async-start(), calls=%async_computation.5 | async-start | bytes 1310720 | tf_op jit(solution)/shard_map/all_gather | solution.py:446
  97.6 8.5 %slice-start.2 = ((s8[8388608]{0:T(1024)(128)(4,1)}), s8[4194304]{0:T(1024)(128)(4,1)S(1)}, s32[]{:S(2)}) async-start(s8[8388608]{0:T(1024)(128)(4,1)} %bitcast.135), calls=%async_computation.9 | async-start | bytes 8388608
  99.7 6.4 %copy-start.18 = (bf16[128,1024]{1,0:T(8,128)(2,1)}, bf16[128,1024]{1,0:T(8,128)(2,1)S(1)}, u32[]{:S(2)}) copy-start(bf16[128,1024]{1,0:T(8,128)(2,1)S(1)} %multiply_convert_fusion.4) | copy-start | bytes 786436
  99.7 6.4 %slice-start.3 = ((s8[8388608]{0:T(1024)(128)(4,1)}), s8[4194304]{0:T(1024)(128)(4,1)S(1)}, s32[]{:S(2)}) async-start(s8[8388608]{0:T(1024)(128)(4,1)} %bitcast.135), calls=%async_computation.10 | async-start | bytes 8388608
  99.7 6.4 %copy-start.12 = (bf16[1,128,1024]{2,1,0:T(8,128)(2,1)S(1)}, bf16[1,128,1024]{2,1,0:T(8,128)(2,1)}, u32[]{:S(2)}) copy-start(bf16[1,128,1024]{2,1,0:T(8,128)(2,1)} %param.33) | copy-start | bytes 786436
  99.7 10.0 %slice-start = ((s8[8388608]{0:T(1024)(128)(4,1)}), s8[4194304]{0:T(1024)(128)(4,1)S(1)}, s32[]{:S(2)}) async-start(s8[8388608]{0:T(1024)(128)(4,1)} %bitcast.133), calls=%async_computation.7 | async-start | bytes 8388608
  114.8 5.2 %copy-start.15 = (bf16[4,128,256]{2,1,0:T(8,128)(2,1)S(1)}, bf16[4,128,256]{2,1,0:T(8,128)(2,1)}, u32[]{:S(2)}) copy-start(bf16[4,128,256]{2,1,0:T(8,128)(2,1)} %copy-done.14) | copy-start | bytes 786436
  116.0 6.3 %copy-start.11 = (bf16[128,4096]{1,0:T(8,128)(2,1)S(1)}, bf16[128,4096]{1,0:T(8,128)(2,1)}, u32[]{:S(2)}) copy-start(bf16[128,4096]{1,0:T(8,128)(2,1)} %get-tuple-element.83) | copy-start | bytes 3145732
  116.0 12.4 %all-to-all-start.1 = ((bf16[2,128,1024]{1,0,2:T(2,128)(2,1)}), bf16[2,128,1024]{1,0,2:T(2,128)(2,1)S(1)}, u32[]{:S(2)}, u32[]{:S(2)}) async-start(bf16[2,128,1024]{1,0,2:T(2,128)(2,1)} %copy.106), calls=%async_computation.1 | async-start | bytes 1048576 | tf_op jit(solution)/shard_map/all_to_all | solution.py:532
  119.6 37.7 %all-gather.6.cloned.1.call-start = ((), (), s32[]{:S(2)}) async-start(), calls=%async_computation.4 | async-start | bytes 2621440 | tf_op jit(solution)/shard_map/all_gather | solution.py:536
  129.8 4.8 %copy-start.7 = (bf16[1536,256]{0,1:T(8,128)(2,1)S(1)}, bf16[1536,256]{0,1:T(8,128)(2,1)}, u32[]{:S(2)}) copy-start(bf16[1536,256]{0,1:T(8,128)(2,1)} %get-tuple-element.72) | copy-start | bytes 2359300
  139.2 4.8 %copy-start.20 = (bf16[512,256]{0,1:T(8,128)(2,1)S(1)}, bf16[512,256]{0,1:T(8,128)(2,1)}, u32[]{:S(2)}) copy-start(bf16[512,256]{0,1:T(8,128)(2,1)} %copy-done.19) | copy-start | bytes 786436
  152.6 4.8 %copy-start.30 = (f32[8,1024]{1,0:T(8,128)}, f32[8,1024]{1,0:T(8,128)S(1)}, u32[]{:S(2)}) copy-start(f32[8,1024]{1,0:T(8,128)S(1)} %scatter.9.refs_13_) | copy-start | bytes 98308
  160.5 5.1 %copy-start.16 = (bf16[2,512,1024]{2,1,0:T(8,128)(2,1)S(1)}, bf16[2,512,1024]{2,1,0:T(8,128)(2,1)}, u32[]{:S(2)}) copy-start(bf16[2,512,1024]{2,1,0:T(8,128)(2,1)} %all-gather.6.cloned.1.call-done) | copy-start | bytes 6291460
  167.1 103.6 %copy-start.9 = (f32[128,1024]{1,0:T(8,128)S(1)}, f32[128,1024]{1,0:T(8,128)}, u32[]{:S(2)}) copy-start(f32[128,1024]{1,0:T(8,128)} %copy-done.8) | copy-start | bytes 1572868
  167.1 103.6 %copy-start.13 = (bf16[1,128,1024]{2,1,0:T(8,128)(2,1)S(1)}, bf16[1,128,1024]{2,1,0:T(8,128)(2,1)}, u32[]{:S(2)}) copy-start(bf16[1,128,1024]{2,1,0:T(8,128)(2,1)} %param.33) | copy-start | bytes 786436
  268.0 6.4 %copy-start.33 = (f32[128,256]{1,0:T(8,128)S(1)}, f32[128,256]{1,0:T(8,128)}, u32[]{:S(2)}) copy-start(f32[128,256]{1,0:T(8,128)} %get-tuple-element.114) | copy-start | bytes 393220
  268.0 7.1 %copy-start.32 = (f32[128,256]{1,0:T(8,128)S(1)}, f32[128,256]{1,0:T(8,128)}, u32[]{:S(2)}) copy-start(f32[128,256]{1,0:T(8,128)} %get-tuple-element.115) | copy-start | bytes 393220
  268.0 7.7 %copy-start.31 = (f32[128,256]{1,0:T(8,128)S(1)}, f32[128,256]{1,0:T(8,128)}, u32[]{:S(2)}) copy-start(f32[128,256]{1,0:T(8,128)} %get-tuple-element.116) | copy-start | bytes 393220
  268.0 8.4 %copy-start.26 = (f32[128,1024]{1,0:T(8,128)S(1)}, f32[128,1024]{1,0:T(8,128)}, u32[]{:S(2)}) copy-start(f32[128,1024]{1,0:T(8,128)} %get-tuple-element.117) | copy-start | bytes 1572868
  268.0 9.2 %copy-start.25 = (f32[512,256]{1,0:T(8,128)S(1)}, f32[512,256]{1,0:T(8,128)}, u32[]{:S(2)}) copy-start(f32[512,256]{1,0:T(8,128)} %get-tuple-element.118) | copy-start | bytes 1572868
  270.7 7.3 %copy-start.27 = (f32[384,256]{1,0:T(8,128)S(1)}, f32[384,256]{1,0:T(8,128)}, u32[]{:S(2)}) copy-start(f32[384,256]{1,0:T(8,128)} %get-tuple-element.119) | copy-start | bytes 1179652
  270.7 8.1 %copy-start.1 = (bf16[1024,1024]{1,0:T(8,128)(2,1)S(1)}, bf16[1024,1024]{1,0:T(8,128)(2,1)}, u32[]{:S(2)}) copy-start(bf16[1024,1024]{1,0:T(8,128)(2,1)} %param.27) | copy-start | bytes 6291460
  (16 other events, 39.8 us)
Sparse Core Ops, SparseCore 0:
  12.0 31.2 all-gather.3
  77.9 23.1 reduce-scatter.1
  102.7 16.7 all-gather.7
  122.4 23.9 all-gather.5
